TPU v7x, 32 devices: a whole 2x2x4 slice. The times are simulated.
32 devices in a mesh: bucket: 8 (over y, x, core), rel: 4 (over z).
Axes of the slice: x: 2, y: 2, z: 4, core: 2. Of those that a mesh axis runs over, the one named last changes fastest.
Arguments:
- src_feat: bfloat16 [2048, 768], P(('bucket', 'rel')), may hold values from -22 to 22
- tgt_feat: bfloat16 [4096, 768], P(('bucket', 'rel')), may hold values from -22 to 22
- enc_weight: bfloat16 [768, 512], replicated, may hold values from -0.21875 to 0.21875
- rel_shift: bfloat16 [12, 512], P('rel'), may hold values from -3 to 3
- edge_src: int32 [8, 4, 4, 768], P('bucket', 'rel'), may hold values from 0 to 255
- edge_tgt: int32 [8, 4, 4, 768], P('bucket', 'rel'), may hold values from 0 to 511
- rel_hot: int32 [8, 4, 4, 3, 768], P('bucket', 'rel'), may hold values from 0 to 1, as said below
- neg_idx: int32 [8, 4, 4, 128], P('bucket', 'rel'), may hold values from 0 to 511
- edge_label: int32 [8, 4, 4, 768], P('bucket', 'rel'), may hold values 0 or 1
Outputs:
- src_grad: float32 [2048, 512], P(('bucket', 'rel'))
- tgt_grad: float32 [4096, 512], P(('bucket', 'rel'))
- rel_grad: float32 [12, 512], P('rel')
- enc_grad: float32 [768, 512], replicated
Inputs may be any that keep to these rules, and one draw needn't show every extreme that they name: `rel_hot`: for each edge exactly one of the three entries is 1.
All inputs are finite; a program needn't handle non-finite values. No bound on the sum of `edge_label` on one device may be relied on, other than what follows from the above.
Results may differ from a plain program's by a relative error of at most 0.00065.
The roundings to bfloat16 on the way count: a program that leaves them out, or rounds other values in their place, can miss the bound.
Values may be sent and summed in bfloat16 or wider, within the bound.
No kernel may reach another device: no remote copies, remote signals or barrier semaphores. Data moves between devices by JAX's collectives and lax.ppermute only.
A program may use at most 64 MiB of HBM per device.

v0:
```python
import functools

import jax
import jax.numpy as jnp
from jax import lax
from jax.experimental import pallas as pl
from jax.experimental.pallas import tpu as pltpu
from jax.sharding import PartitionSpec as P


CHUNKS = 2
LABELLED = 1024.0
LOG2E = 1.4426950408889634
SLOT_OF = (0, 1, 3, 2)
APART = (0, 2, 1, 3)
NT = (((1,), (1,)), ((), ()))
NN = (((1,), (0,)), ((), ()))
F32 = jnp.float32
BF16 = jnp.bfloat16
VMEM = pl.BlockSpec(memory_space=pltpu.VMEM)
ANY = pl.BlockSpec(memory_space=pl.ANY)


def dot(a, b, dims):
    return lax.dot_general(a, b, dims, preferred_element_type=F32)


def call(body, outs, ins, in_specs=None, scratch=(), flops=0):
    moved = sum(x.size * x.dtype.itemsize for x in ins)
    moved += sum(o.size * o.dtype.itemsize for o in outs)
    return pl.pallas_call(
        body,
        out_shape=tuple(outs),
        in_specs=in_specs or [VMEM] * len(ins),
        out_specs=tuple(VMEM for _ in outs),
        scratch_shapes=scratch,
        cost_estimate=pl.CostEstimate(flops=int(flops), bytes_accessed=int(moved), transcendentals=0),
    )(*ins)


def shaped(shape, dtype=F32):
    return jax.ShapeDtypeStruct(tuple(shape), dtype)


def field_starts(edges, negs):
    starts, at = {}, 0
    for key, size in (
        ("src", edges), ("tlo", edges), ("thi", edges), ("rel", edges), ("lab", edges), ("nlo", negs), ("nhi", negs),
    ):
        starts[key] = (at, size)
        at += size
    return starts, at


def task_rows(edges, negs, width):
    total = field_starts(edges, negs)[1]
    return -(-total // width // 8) * 8 if total % width == 0 else (-(-(-(-total // width)) // 8)) * 8


def pack(fields, rows, src, tgt, rel, neg, lab, flat):
    slots = src.shape[2]
    width = flat.shape[1]
    flat[...] = jnp.zeros_like(flat)
    for m in range(slots):
        tgt_f = tgt[0, 0, m : m + 1, :].astype(F32)
        neg_f = neg[0, 0, m : m + 1, :].astype(F32)
        t_hi = jnp.floor(tgt_f * (1.0 / 256))
        n_hi = jnp.floor(neg_f * (1.0 / 256))
        values = {
            "src": src[0, 0, m : m + 1, :].astype(F32), "tlo": tgt_f - 256.0 * t_hi, "thi": t_hi,
            "rel": rel[m : m + 1, :].astype(F32), "lab": lab[0, 0, m : m + 1, :].astype(F32),
            "nlo": neg_f - 256.0 * n_hi, "nhi": n_hi,
        }
        for key, (at, size) in fields.items():
            done = 0
            while done < size:
                row, col = divmod(at + done, width)
                n = min(width - col, size - done)
                flat[m * rows + row : m * rows + row + 1, col : col + n] = values[key][:, done : done + n]
                done += n


def first_body(fields, rows, src_feat, weight, src, tgt, rel, neg, lab, shift, out, act, flat):
    pack(fields, rows, src, tgt, rel, neg, lab, flat)
    n = src_feat.shape[0]
    value = jnp.tanh(dot(src_feat[...], weight[...], NN))
    act[...] = value
    out[:n, :] = value.astype(BF16)
    tasks = flat.shape[0]
    out[n : n + tasks, :] = flat[...].astype(BF16)
    out[n + tasks :, :] = jnp.zeros_like(out[n + tasks :, :])
    out[n + tasks : n + tasks + shift.shape[0], :] = shift[...]


def take(block, fields, key):
    at, size = fields[key]
    width = block.shape[1]
    pieces, done = [], 0
    while done < size:
        row, col = divmod(at + done, width)
        n = min(width - col, size - done)
        pieces.append(block[row : row + 1, col : col + n])
        done += n
    return pieces[0] if len(pieces) == 1 else jnp.concatenate(pieces, axis=1)


def wrapped(value, base, count):
    moved = value - base
    return jnp.where(moved < 0, moved + count, moved)


def one_hot(rows, ids, value=None):
    one = jnp.full(ids.shape, 1.0, BF16) if value is None else value.astype(BF16)
    pieces = []
    for base in range(0, rows, 256):
        n = min(256, rows - base)
        local = jnp.where((ids >= base) & (ids < base + n), ids - base, -1.0).astype(BF16)
        iota = lax.broadcasted_iota(jnp.int32, (n, ids.shape[1]), 0).astype(F32).astype(BF16)
        pieces.append(jnp.where(iota == local, one, jnp.zeros_like(one)))
    return pieces[0] if len(pieces) == 1 else jnp.concatenate(pieces, axis=0)


def own_quarter(size):
    me = lax.axis_index("bucket")
    return (me & 1) * 2 + ((me >> (size.bit_length() - 2)) & 1)


def own_half():
    return (lax.axis_index("bucket") >> 1) & 1


def aligned(number, size, base=0):
    return pl.ds(pl.multiple_of(base + number * size, size), size)


def prepare_body(size, *refs):
    src, tgt, weight, (act, src_turned, tgt_turned, src_held, tgt_held) = refs[:4], refs[4:8], refs[8], refs[9:]
    me = own_quarter(size)
    for feats, held, turned in ((src, src_held, src_turned), (tgt, tgt_held, tgt_turned)):
        for j, x in enumerate(feats):
            held[aligned(me ^ APART[j], x.shape[0]), :] = x[...]
        turned[...] = held[...].astype(F32).T.astype(BF16)
    act[...] = jnp.tanh(dot(tgt_held[...], weight[:, aligned(me, act.shape[1])], NN))


def spread(pieces, targets):
    own, plus, minus, far_a, far_b = pieces
    copies = []
    half = far_a.shape[0]
    for place, parts in ((0, ((own, 0),)), (1, ((plus, 0),)), (2, ((far_a, 0), (far_b, half))), (3, ((minus, 0),))):
        for lo, hi, ref in targets(place):
            for part, base in parts:
                a, b = max(lo, base), min(hi, base + part.shape[0])
                if a < b:
                    copies.append((part.at[pl.ds(a - base, b - a)], ref.at[pl.ds(a - lo, b - a)]))
    return copies


def weights_of(scores, coded, pairs, scale):
    sig = 1.0 / (1.0 + jnp.exp2(scores * (-scale * LOG2E)))
    labels = jnp.floor(coded * (1.0 / LABELLED))
    edges = coded - (LABELLED - 1.0) * labels
    return edges * sig - labels + pairs * sig.astype(BF16).astype(F32)


def meets_body(cfg, own, plus, minus, far_a, far_b, f_own, f_low, f_high, f_far, weights, *refs):
    fields, rows, s_rows, t_rows, n_rel, scale, groups, negs, size = cfg
    t_outs, s_outs = refs[:4], refs[4:8]
    src, idx, feats, weight_v, tgt, query_a, query_b, parts_a, parts_b, acc, w_src, w_rel, total, sems = refs[8:]
    ring = lax.axis_index("rel")
    tasks = idx.shape[1] - 16

    def places(place):
        return (0, s_rows, src.at[pl.ds(place * s_rows, s_rows)]), (s_rows, own.shape[0], idx.at[place])

    copies = [(weights, weight_v)]
    copies += [(x, feats.at[pl.ds(j * t_rows, t_rows)]) for j, x in enumerate((f_own, f_low, f_high, f_far))]
    early = len(copies)
    copies += spread((own, plus, minus, far_a, far_b), places)
    copies = [pltpu.make_async_copy(a, b, sems.at[i]) for i, (a, b) in enumerate(copies)]
    for c in copies:
        c.start()
    for c in copies[:early]:
        c.wait()
    tgt[...] = jnp.tanh(dot(feats[...], weight_v[...], NN)).astype(BF16)
    for c in copies[early:]:
        c.wait()
    for ref in (acc, w_src, w_rel, query_b, parts_b):
        ref[...] = jnp.zeros_like(ref)
    all_src = src.shape[0]
    all_tgt = t_rows * groups
    src_base = (ring * s_rows).astype(F32)
    tgt_base = (ring * t_rows).astype(F32)
    lane = lax.broadcasted_iota(jnp.int32, (t_rows, w_rel.shape[1]), 1)

    def one_group(group, query, parts):
        shift = idx[group, tasks : tasks + 16, :]
        place = lax.rem(group + ring, groups) * n_rel
        for k in range(n_rel):
            rows_k = src[...] + shift[k : k + 1, :]
            query[k * all_src : (k + 1) * all_src, :] = rows_k
            query[(n_rel + k) * all_src : (n_rel + k + 1) * all_src, :] = rows_k
        scores = dot(tgt[...], query[: n_rel * all_src, :], NT)
        for j, slot in enumerate(SLOT_OF):
            block = idx[group, slot * rows : (slot + 1) * rows, :].astype(F32)
            who = wrapped(take(block, fields, "src"), src_base, float(all_src))
            rel = take(block, fields, "rel")
            ids = wrapped(take(block, fields, "thi") * 256.0 + take(block, fields, "tlo"), tgt_base, float(all_tgt))
            weight = 1.0 + (LABELLED - 1.0) * take(block, fields, "lab")
            left = [one_hot(t_rows, jnp.where(rel == float(k), ids, -1.0), weight) for k in range(n_rel)]
            left.append(one_hot(16, rel))
            counts = dot(jnp.concatenate(left, axis=0), one_hot(all_src, who), NT)
            neg = wrapped(take(block, fields, "nhi") * 256.0 + take(block, fields, "nlo"), tgt_base, float(all_tgt))
            neg_count = jnp.sum(one_hot(t_rows, neg).astype(F32), axis=1, keepdims=True) * (1.0 / negs)
            mine = slice(j * t_rows, (j + 1) * t_rows)
            part, line = None, jnp.zeros((t_rows, w_rel.shape[1]), F32)
            for k in range(n_rel):
                top = k * t_rows
                each = n_rel * t_rows + k
                lanes = slice(k * all_src, (k + 1) * all_src)
                value = weights_of(
                    scores[mine, lanes], counts[top : top + t_rows, :], neg_count * counts[each : each + 1, :], scale
                )
                high = value.astype(BF16)
                parts[mine, lanes] = high
                lanes = slice((n_rel + k) * all_src, (n_rel + k + 1) * all_src)
                parts[mine, lanes] = (value - high.astype(F32)).astype(BF16)
                part = value if part is None else part + value
                line = jnp.where(lane == place + k, jnp.sum(value, axis=1, keepdims=True), line)
            w_src[mine, :] += part
            w_rel[mine, :] += line

    def step(pair, carry):
        one_group(2 * pair, query_a, parts_a)
        acc[...] += dot(parts_b[...], query_b[...], NN)
        one_group(2 * pair + 1, query_b, parts_b)
        acc[...] += dot(parts_a[...], query_a[...], NN)
        return carry

    lax.fori_loop(0, groups // 2, step, 0)
    acc[...] += dot(parts_b[...], query_b[...], NN)
    whole = jnp.concatenate([w_src[...].T, w_rel[...].T[:16, :]], axis=0)
    high = whole.astype(BF16)
    low = (whole - high.astype(F32)).astype(BF16)
    total[...] = scale * (dot(high, tgt[...], NN) + dot(low, tgt[...], NN))
    for r, out in enumerate(s_outs):
        place = lax.rem((ring ^ r) - ring + groups, groups)
        out[...] = total[aligned(place, s_rows), :]
    me = own_quarter(size)
    for i, out in enumerate(t_outs):
        lanes = aligned(me ^ APART[i], out.shape[1])
        for j in range(4):
            out[aligned(me ^ APART[j], t_rows), :] = scale * acc[j * t_rows : (j + 1) * t_rows, lanes]
        out[4 * t_rows :, :] = total[all_src:, lanes]


def source_body(size, a, b, c, d, act, grad, *outs):
    value = (a[...] + b[...]) + (c[...] + d[...])
    grad[...] = value
    d = (value * (1.0 - act[...] * act[...])).astype(BF16)
    wide = outs[0].shape[1]
    me = own_quarter(size)
    for a in range(4):
        for j, out in enumerate(outs):

            @pl.when((me ^ APART[j]) == a)
            def _():
                out[...] = d[:, a * wide : (a + 1) * wide]


def target_body(size, keep, recv, last, act, turned, *outs):
    parts, rows = outs[:2], outs[2:]
    value = (keep[...] + recv[...]) + last[...]
    n = act.shape[0]
    d = (value[:n, :] * (1.0 - act[...] * act[...])).astype(BF16)
    block = turned.shape[0] // 2
    for r, out in enumerate(parts):
        out[:block, :] = dot(turned[aligned(own_half() ^ r, block), :], d, NN)
        out[block:, :] = value[n:, :]
    me = own_quarter(size)
    for a in range(4):
        for j, out in enumerate(rows):

            @pl.when((me ^ APART[j]) == a)
            def _():
                out[...] = value[a * (n // 4) : (a + 1) * (n // 4), :]


def join_body(size, keep_in, send_in, turned, *refs):
    pieces, outs, held = refs[:4], refs[4:-1], refs[-1]
    n = pieces[0].shape[0]
    me = own_quarter(size)
    for j, x in enumerate(pieces):
        held[aligned(me ^ APART[j], n), :] = x[...]
    block = turned.shape[0] // 2
    part = block // CHUNKS
    for r, x in enumerate((keep_in, send_in)):
        added = dot(turned[aligned(own_half() ^ r, block), :], held[...], NN)
        for c, out in enumerate(outs[r * CHUNKS : (r + 1) * CHUNKS]):
            out[:part, :] = x[c * part : (c + 1) * part, :] + added[c * part : (c + 1) * part, :]
            if c == 0:
                out[part:, :] = x[block:, :]


def rows_body(size, *refs):
    parts, (grad,) = refs[:4], refs[4:]
    me = own_quarter(size)
    for j, x in enumerate(parts):
        grad[:, aligned(me ^ APART[j], x.shape[1])] = x[...]


def place_body(size, *refs):
    blocks, (enc_grad, rel_grad) = refs[:-2], refs[-2:]
    part = enc_grad.shape[0] // 2 // CHUNKS
    me = own_quarter(size)
    n_rel = rel_grad.shape[0]
    for at, x in enumerate(blocks):
        r, c, j = at // (4 * CHUNKS), at // 4 % CHUNKS, at % 4
        lanes = aligned(me ^ APART[j], x.shape[1])
        enc_grad[aligned((own_half() ^ r) * CHUNKS + c, part), lanes] = x[:part, :]
        if r == 0 and c == 0:
            for k in range(n_rel):
                rel_grad[k : k + 1, lanes] = x[pl.ds(part + lax.axis_index("rel") * n_rel + k, 1), :]


def shards(src_feat, tgt_feat, enc_weight, rel_shift, edge_src, edge_tgt, rel_hot, neg_idx, edge_label):
    buckets = lax.axis_size("bucket")
    groups = lax.axis_size("rel")
    half = buckets // 2
    s_rows, t_rows = src_feat.shape[0], tgt_feat.shape[0]
    feat, emb = enc_weight.shape
    slots, edges = edge_src.shape[2:]
    negs = neg_idx.shape[3]
    n_rel = rel_hot.shape[3]
    fields, _ = field_starts(edges, negs)
    rows = task_rows(edges, negs, emb)
    cfg = (fields, rows, s_rows, t_rows, n_rel, emb**-0.5, groups, negs, buckets)
    wide = emb // 4

    def met(x, mask):
        return lax.ppermute(x, "bucket", [(i, i ^ mask) for i in range(buckets)])

    def ring(x, step):
        return lax.ppermute(x, "rel", [(i, (i - step) % groups) for i in range(groups)])

    def crossed(x, mask):
        return lax.ppermute(x, "rel", [(i, i ^ mask) for i in range(groups)])

    def around(x):
        cut_at = x.shape[0] // 2
        plus, minus = ring(x, 1), ring(x, -1)
        return x, plus, minus, ring(plus[:cut_at], 1), ring(minus[cut_at:], -1)

    def shared(parts):
        return [parts[0], met(parts[1], 1), met(parts[2], half), met(parts[3], half + 1)]

    which = sum(k * rel_hot[0, 0, :, k, :] for k in range(1, n_rel))
    own, s_act = call(
        functools.partial(first_body, fields, rows),
        [shaped((s_rows + slots * rows + 16, emb), BF16), shaped((s_rows, emb))],
        [src_feat, enc_weight, edge_src, edge_tgt, which, neg_idx, edge_label, rel_shift],
        scratch=[pltpu.VMEM((slots * rows, emb), F32)],
        flops=2 * s_rows * feat * emb,
    )
    first = around(own)

    def fetched(x):
        high = met(x, half)
        return [x, met(x, 1), high, met(high, 1)]

    t_feats, s_feats = fetched(tgt_feat), fetched(src_feat)
    queries = n_rel * groups * s_rows
    t_feats, s_feats = lax.optimization_barrier((t_feats, s_feats))
    parts = call(
        functools.partial(meets_body, cfg),
        [shaped((4 * t_rows + 16, wide))] * 4 + [shaped((s_rows, emb))] * groups,
        [*first, *t_feats, enc_weight],
        in_specs=[ANY] * 10,
        scratch=[
            pltpu.VMEM((groups * s_rows, emb), BF16),
            pltpu.VMEM((groups, slots * rows + 16, emb), BF16),
            pltpu.VMEM((4 * t_rows, feat), BF16),
            pltpu.VMEM((feat, emb), BF16),
            pltpu.VMEM((4 * t_rows, emb), BF16),
            pltpu.VMEM((2 * queries, emb), BF16),
            pltpu.VMEM((2 * queries, emb), BF16),
            pltpu.VMEM((4 * t_rows, 2 * queries), BF16),
            pltpu.VMEM((4 * t_rows, 2 * queries), BF16),
            pltpu.VMEM((4 * t_rows, emb), F32),
            pltpu.VMEM((4 * t_rows, groups * s_rows), F32),
            pltpu.VMEM((4 * t_rows, 128), F32),
            pltpu.VMEM((groups * s_rows + 16, emb), F32),
            pltpu.SemaphoreType.DMA((32,)),
        ],
        flops=12e9,
    )
    t_parts, s_parts = parts[:4], parts[4:]
    s_parts = [s_parts[0], *(crossed(s_parts[mask], mask) for mask in range(1, groups))]
    t_recv, t_next = met(t_parts[1], 1), met(t_parts[3], 1)
    t_last = met(t_parts[2] + t_next, half)
    s_feats, t_recv = lax.optimization_barrier((s_feats, t_recv))
    act, s_turned, t_turned = call(
        functools.partial(prepare_body, buckets),
        [shaped((4 * t_rows, wide)), shaped((feat, 4 * s_rows), BF16), shaped((feat, 4 * t_rows), BF16)],
        [*s_feats, *t_feats, enc_weight],
        scratch=[pltpu.VMEM((4 * s_rows, feat), BF16), pltpu.VMEM((4 * t_rows, feat), BF16)],
        flops=8 * t_rows * feat * wide,
    )
    s_parts, act = lax.optimization_barrier((s_parts, act))
    part = feat // 2
    src_grad, *d_parts = call(
        functools.partial(source_body, buckets),
        [shaped((s_rows, emb))] + [shaped((s_rows, wide), BF16)] * 4,
        [*s_parts, s_act],
    )
    d_parts, t_last = lax.optimization_barrier((d_parts, t_last))
    keep, send, *g_parts = call(
        functools.partial(target_body, buckets),
        [shaped((part + 16, wide))] * 2 + [shaped((t_rows, wide))] * 4,
        [t_parts[0], t_recv, t_last, act, t_turned],
        flops=8 * t_rows * feat * wide,
    )
    d_parts = shared(d_parts)
    piece = part // CHUNKS
    sizes = [shaped((piece + (16 if c == 0 else 0), wide)) for c in range(CHUNKS)] * 2
    halves = call(
        functools.partial(join_body, buckets),
        sizes,
        [keep, send, s_turned, *d_parts],
        scratch=[pltpu.VMEM((4 * s_rows, wide), BF16)],
        flops=8 * s_rows * feat * wide,
    )
    got = [met(x, 2) for x in halves[CHUNKS:]]
    g_parts, got[0] = lax.optimization_barrier((shared(g_parts), got[0]))
    (tgt_grad,) = call(functools.partial(rows_body, buckets), [shaped((t_rows, emb))], g_parts)
    blocks = [[], []]
    for c in range(CHUNKS):
        joint = halves[c] + got[c]
        for bit in range(2, buckets.bit_length() - 2):
            joint = joint + met(joint, 1 << bit)
        for mask in (1, 3) if c % 2 == 0 else (3, 1):
            joint = joint + crossed(joint, mask)
            if c == 0 and mask == 1:
                tgt_grad, joint = lax.optimization_barrier((tgt_grad, joint))
        for r, same in ((0, [joint, met(joint, half)]), (1, [met(joint, 2), met(joint, half + 2)])):
            other = [met(x, 1) for x in same]
            blocks[r] += [same[0], other[0], same[1], other[1]]
    enc_grad, rel_grad = call(
        functools.partial(place_body, buckets), [shaped((feat, emb)), shaped((n_rel, emb))], [*blocks[0], *blocks[1]]
    )
    return (src_grad, tgt_grad, rel_grad, enc_grad)


def solution(mesh):
    in_specs = (
        P(("bucket", "rel"), None),
        P(("bucket", "rel"), None),
        P(),
        P("rel", None),
        P("bucket", "rel", None, None),
        P("bucket", "rel", None, None),
        P("bucket", "rel", None, None, None),
        P("bucket", "rel", None, None),
        P("bucket", "rel", None, None),
    )
    out_specs = (P(("bucket", "rel"), None), P(("bucket", "rel"), None), P("rel", None), P())

    return jax.shard_map(shards, mesh=mesh, in_specs=in_specs, out_specs=out_specs, check_vma=False)
```

profile of v0, /device:TPU:0, one launch (start us, length us, event | category | flops | bytes accessed | tf_op | source)
XLA Modules:
  0.0 111.6 jit_solution(6702341335626297661)
XLA Ops:
  0.6 3.1 %collective-permute-start.8 = (bf16[64,768]{1,0:T(8,128)(2,1)}, bf16[64,768]{1,0:T(8,128)(2,1)S(1)}, u32[]{:S(2)}, u32[]{:S(2)}) collective-permute-start(bf16[64,768]{1,0:T(8,128)(2,1)} %refs_0_), channel_id=1, source_target_pairs={{0,16},{4,20},{8,24},{12,28},{16,0},{20,4},{24,8},{28,12},{1,17},{... | collective-permute-start | bytes 294920 | tf_op jit(solution)/shard_map/ppermute | solution.py:341
  3.8 1.3 %add_bitcast_fusion.rel = s32[4,768]{1,0:T(4,128)} fusion(s32[1,1,4,3,768]{4,2,3,1,0:T(4,128)} %param.15), kind=kLoop, calls=%fused_computation | loop fusion | flops 6144 | bytes 36864 | tf_op jit(solution)/shard_map/add | solution.py:357
  5.1 2.1 %shard_map.120 = (bf16[112,512]{1,0:T(8,128)(2,1)}, f32[64,512]{1,0:T(8,128)}) custom-call(bf16[64,768]{1,0:T(8,128)(2,1)} %refs_0_, bf16[768,512]{1,0:T(8,128)(2,1)} %refs_8_.1, s32[1,1,4,768]{3,2,1,0:T(4,128)} %src.1, s32[1,1,4,768]{3,2,1,0:T(4,128)} %tgt.1, s32[4,768]{1,0:T(4,128)} %add_bitcast_fusion.rel, s32[1,1,4,128]{3,2,1,0:T(4,128)} %neg.1, ...), custom_call_target="tpu_custom_call" | custom-call | flops 50331648 | bytes 1184768 | tf_op jit(solution)/shard_map/pallas_call | solution.py:31
  7.2 2.0 %collective-permute-start.1 = (bf16[112,512]{1,0:T(8,128)(2,1)}, bf16[112,512]{1,0:T(8,128)(2,1)S(1)}, u32[]{:S(2)}, u32[]{:S(2)}) collective-permute-start(bf16[112,512]{1,0:T(8,128)(2,1)} %get-tuple-element.64.own), channel_id=1, source_target_pairs={{0,1},{1,2},{2,3},{3,0},{4,5},{5,6},{6,7},{7,4},{8,9},{9,10},{10,1... | collective-permute-start | bytes 344072 | tf_op jit(solution)/shard_map/ppermute | solution.py:344
  9.2 1.7 %collective-permute-done.5.f_high.refs_6_ = bf16[128,768]{1,0:T(8,128)(2,1)S(1)} collective-permute-done((bf16[128,768]{1,0:T(8,128)(2,1)}, bf16[128,768]{1,0:T(8,128)(2,1)S(1)}, u32[]{:S(2)}, u32[]{:S(2)}) %collective-permute-start.5) | collective-permute-done | bytes 196640 | tf_op jit(solution)/shard_map/ppermute | solution.py:341
  10.9 3.9 %collective-permute-start = (bf16[112,512]{1,0:T(8,128)(2,1)}, bf16[112,512]{1,0:T(8,128)(2,1)S(1)}, u32[]{:S(2)}, u32[]{:S(2)}) collective-permute-start(bf16[112,512]{1,0:T(8,128)(2,1)} %get-tuple-element.64.own), channel_id=1, source_target_pairs={{0,3},{1,0},{2,1},{3,2},{4,7},{5,4},{6,5},{7,6},{8,11},{9,8},{10,9... | collective-permute-start | bytes 344072 | tf_op jit(solution)/shard_map/ppermute | solution.py:344
  14.8 0.2 collective-permute-start.7
  15.1 0.3 collective-permute-start.9
  15.3 2.9 %collective-permute-done.plus = bf16[112,512]{1,0:T(8,128)(2,1)S(1)} collective-permute-done((bf16[112,512]{1,0:T(8,128)(2,1)}, bf16[112,512]{1,0:T(8,128)(2,1)S(1)}, u32[]{:S(2)}, u32[]{:S(2)}) %collective-permute-start) | collective-permute-done | bytes 114720 | tf_op jit(solution)/shard_map/ppermute | solution.py:344
  18.2 0.4 collective-permute-start.3
  18.6 3.9 %collective-permute-start.2 = (bf16[56,512]{1,0:T(8,128)(2,1)S(1)}, bf16[56,512]{1,0:T(8,128)(2,1)S(1)}, u32[]{:S(2)}, u32[]{:S(2)}) collective-permute-start(bf16[56,512]{1,0:T(8,128)(2,1)S(1)} %slice.16), channel_id=1, source_target_pairs={{0,3},{1,0},{2,1},{3,2},{4,7},{5,4},{6,5},{7,6},{8,11},{9,8},{10,9... | collective-permute-start | bytes 172040 | tf_op jit(solution)/shard_map/ppermute | solution.py:344
  22.5 2.1 %collective-permute-done.3.far_b = bf16[56,512]{1,0:T(8,128)(2,1)S(1)} collective-permute-done((bf16[56,512]{1,0:T(8,128)(2,1)S(1)}, bf16[56,512]{1,0:T(8,128)(2,1)S(1)}, u32[]{:S(2)}, u32[]{:S(2)}) %collective-permute-start.3) | collective-permute-done | bytes 57376 | tf_op jit(solution)/shard_map/ppermute | solution.py:344
  24.7 0.6 copy-done.35
  25.3 0.6 copy-done.36
  25.9 15.3 %shard_map.121 = (f32[528,128]{1,0:T(8,128)}, f32[528,128]{1,0:T(8,128)}, f32[528,128]{1,0:T(8,128)}, f32[528,128]{1,0:T(8,128)}, f32[64,512]{1,0:T(8,128)}, /*i...) custom-call(bf16[112,512]{1,0:T(8,128)(2,1)} %get-tuple-element.64.own, bf16[112,512]{1,0:T(8,128)(2,1)} %copy-done.31, ...), custom_call_target="tpu_custom_call" | custom-call | flops 12000000000 | bytes 3637248 | tf_op jit(solution)/shard_map/pallas_call | solution.py:31
  41.3 0.5 collective-permute-start.13
  41.8 1.2 %collective-permute-done.14 = f32[528,128]{1,0:T(8,128)S(1)} collective-permute-done((f32[528,128]{1,0:T(8,128)}, f32[528,128]{1,0:T(8,128)S(1)}, u32[]{:S(2)}, u32[]{:S(2)}) %collective-permute-start.14) | collective-permute-done | bytes 270368 | tf_op jit(solution)/shard_map/ppermute | solution.py:341
  43.0 1.0 add.28
  44.0 1.5 %collective-permute-start.15 = (f32[528,128]{1,0:T(8,128)S(1)}, f32[528,128]{1,0:T(8,128)S(1)}, u32[]{:S(2)}, u32[]{:S(2)}) collective-permute-start(f32[528,128]{1,0:T(8,128)S(1)} %add.28), channel_id=1, source_target_pairs={{0,16},{4,20},{8,24},{12,28},{16,0},{20,4},{24,8},{28,12},{1,17},{... | collective-permute-start | bytes 811016 | tf_op jit(solution)/shard_map/ppermute | solution.py:341
  45.5 0.7 collective-permute-start.10
  46.2 3.1 %collective-permute-start.11 = (f32[64,512]{1,0:T(8,128)}, f32[64,512]{1,0:T(8,128)S(1)}, u32[]{:S(2)}, u32[]{:S(2)}) collective-permute-start(f32[64,512]{1,0:T(8,128)} %get-tuple-element.71), channel_id=1, source_target_pairs={{0,2},{1,3},{2,0},{3,1},{4,6},{5,7},{6,4},{7,5},{8,10},{9,11},{10,... | collective-permute-start | bytes 393224 | tf_op jit(solution)/shard_map/ppermute | solution.py:347
  49.3 0.6 collective-permute-start.12
  49.9 3.1 %shard_map.122 = (f32[512,128]{1,0:T(8,128)}, bf16[768,256]{1,0:T(8,128)(2,1)}, bf16[768,512]{1,0:T(8,128)(2,1)}) custom-call(bf16[64,768]{1,0:T(8,128)(2,1)} %refs_0_, bf16[64,768]{1,0:T(8,128)(2,1)} %copy-done.25, bf16[64,768]{1,0:T(8,128)(2,1)} %copy-done.24, bf16[64,768]{1,0:T(8,128)(2,1)} %copy-done.26, bf16[128,768]{1,0:T(8,128)(2,1)} %refs_4_, ...), custom_call_target="tpu_custom_call" | custom-call | flops 100663296 | bytes 3407872 | tf_op jit(solution)/shard_map/pallas_call | solution.py:31
  53.0 6.4 %collective-permute-done.11.c = f32[64,512]{1,0:T(8,128)S(1)} collective-permute-done((f32[64,512]{1,0:T(8,128)}, f32[64,512]{1,0:T(8,128)S(1)}, u32[]{:S(2)}, u32[]{:S(2)}) %collective-permute-start.11) | collective-permute-done | bytes 131104 | tf_op jit(solution)/shard_map/ppermute | solution.py:347
  59.5 0.6 copy-done.8
  60.2 1.9 %shard_map.123 = (f32[64,512]{1,0:T(8,128)}, bf16[64,128]{1,0:T(8,128)(2,1)}, bf16[64,128]{1,0:T(8,128)(2,1)}, bf16[64,128]{1,0:T(8,128)(2,1)}, bf16[64,128]{1,0:T(8,128)(2,1)}) custom-call(f32[64,512]{1,0:T(8,128)} %get-tuple-element.83.a, f32[64,512]{1,0:T(8,128)} %copy-done.7, f32[64,512]{1,0:T(8,128)} %copy-done.8, f32[64,512]{1,0:T(8,128)} %copy-done.9, ...), custom_call_target="tpu_custom_call" | custom-call | bytes 851968 | tf_op jit(solution)/shard_map/pallas_call | solution.py:31
  62.2 0.7 collective-permute-start.20
  62.9 1.2 %collective-permute-start.21 = (bf16[64,128]{1,0:T(8,128)(2,1)}, bf16[64,128]{1,0:T(8,128)(2,1)S(1)}, u32[]{:S(2)}, u32[]{:S(2)}) collective-permute-start(bf16[64,128]{1,0:T(8,128)(2,1)} %get-tuple-element.110), channel_id=1, source_target_pairs={{0,20},{4,16},{8,28},{12,24},{16,4},{20,0},{24,12},{28,8},{1,21},{... | collective-permute-start | bytes 49160 | tf_op jit(solution)/shard_map/ppermute | solution.py:341
  64.0 2.9 %shard_map.124 = (f32[400,128]{1,0:T(8,128)}, f32[400,128]{1,0:T(8,128)}, f32[128,128]{1,0:T(8,128)}, f32[128,128]{1,0:T(8,128)}, f32[128,128]{1,0:T(8,128)}, /*index=5*/f32[128,128]{1,0:T(8,128)}) custom-call(f32[528,128]{1,0:T(8,128)} %get-tuple-element.89.keep, f32[528,128]{1,0:T(8,128)} %copy-done.2, f32[528,128]{1,0:T(8,128)} %copy-done.3, ...), custom_call_target="tpu_custom_call" | custom-call | flops 100663296 | bytes 2531328 | tf_op jit(solution)/shard_map/pallas_call | solution.py:31
  67.0 0.6 copy-done.32
  67.6 2.2 %shard_map.125 = (f32[208,128]{1,0:T(8,128)}, f32[192,128]{1,0:T(8,128)}, f32[208,128]{1,0:T(8,128)}, f32[192,128]{1,0:T(8,128)}) custom-call(f32[400,128]{1,0:T(8,128)} %get-tuple-element.104.keep_in, f32[400,128]{1,0:T(8,128)} %get-tuple-element.105.send_in, bf16[768,256]{1,0:T(8,128)(2,1)} %get-tuple-element.106.turned, ...), custom_call_target="tpu_custom_call" | custom-call | flops 50331648 | bytes 1277952 | tf_op jit(solution)/shard_map/pallas_call | solution.py:31
  69.8 1.5 %collective-permute-start.28 = (f32[192,128]{1,0:T(8,128)}, f32[192,128]{1,0:T(8,128)S(1)}, u32[]{:S(2)}, u32[]{:S(2)}) collective-permute-start(f32[192,128]{1,0:T(8,128)} %get-tuple-element.121), channel_id=1, source_target_pairs={{0,8},{4,12},{8,0},{12,4},{16,24},{20,28},{24,16},{28,20},{1,9},{5... | collective-permute-start | bytes 294920 | tf_op jit(solution)/shard_map/ppermute | solution.py:341
  71.3 0.5 collective-permute-start.22
  71.9 3.9 %collective-permute-done.28 = f32[192,128]{1,0:T(8,128)S(1)} collective-permute-done((f32[192,128]{1,0:T(8,128)}, f32[192,128]{1,0:T(8,128)S(1)}, u32[]{:S(2)}, u32[]{:S(2)}) %collective-permute-start.28) | collective-permute-done | bytes 98336 | tf_op jit(solution)/shard_map/ppermute | solution.py:341
  75.7 0.9 add.32
  76.6 2.6 %collective-permute-start.29 = (f32[192,128]{1,0:T(8,128)S(1)}, f32[192,128]{1,0:T(8,128)S(1)}, u32[]{:S(2)}, u32[]{:S(2)}) collective-permute-start(f32[192,128]{1,0:T(8,128)S(1)} %add.32), channel_id=1, source_target_pairs={{0,3},{1,2},{2,1},{3,0},{4,7},{5,6},{6,5},{7,4},{8,11},{9,10},{10,... | collective-permute-start | bytes 294920 | tf_op jit(solution)/shard_map/ppermute | solution.py:347
  79.2 0.6 collective-permute-start.17
  79.9 1.2 %collective-permute-start.18 = (f32[128,128]{1,0:T(8,128)}, f32[128,128]{1,0:T(8,128)S(1)}, u32[]{:S(2)}, u32[]{:S(2)}) collective-permute-start(f32[128,128]{1,0:T(8,128)} %get-tuple-element.103), channel_id=1, source_target_pairs={{0,20},{4,16},{8,28},{12,24},{16,4},{20,0},{24,12},{28,8},{1,21},{... | collective-permute-start | bytes 196616 | tf_op jit(solution)/shard_map/ppermute | solution.py:341
  81.1 3.3 %collective-permute-done.17.refs_2_ = f32[128,128]{1,0:T(8,128)S(1)} collective-permute-done((f32[128,128]{1,0:T(8,128)}, f32[128,128]{1,0:T(8,128)S(1)}, u32[]{:S(2)}, u32[]{:S(2)}) %collective-permute-start.17) | collective-permute-done | bytes 65568 | tf_op jit(solution)/shard_map/ppermute | solution.py:341
  84.4 0.5 collective-permute-done.18.refs_3_
  84.9 0.9 add.29
  85.8 1.2 %collective-permute-start.23 = (f32[208,128]{1,0:T(8,128)S(1)}, f32[208,128]{1,0:T(8,128)S(1)}, u32[]{:S(2)}, u32[]{:S(2)}) collective-permute-start(f32[208,128]{1,0:T(8,128)S(1)} %add.29), channel_id=1, source_target_pairs={{0,1},{1,0},{2,3},{3,2},{4,5},{5,4},{6,7},{7,6},{8,9},{9,8},{10,11... | collective-permute-start | bytes 319496 | tf_op jit(solution)/shard_map/ppermute | solution.py:347
  87.1 0.9 collective-permute-start.30
  88.0 1.7 %shard_map.126 = f32[128,512]{1,0:T(8,128)} custom-call(f32[128,128]{1,0:T(8,128)} %get-tuple-element.112.refs_0_, f32[128,128]{1,0:T(8,128)} %copy-done.27, f32[128,128]{1,0:T(8,128)} %copy-done.28, f32[128,128]{1,0:T(8,128)} %copy-done.29), custom_call_target="tpu_custom_call" | custom-call | bytes 524288 | tf_op jit(solution)/shard_map/pallas_call | solution.py:31
  89.7 2.0 %collective-permute-done.23 = f32[208,128]{1,0:T(8,128)S(1)} collective-permute-done((f32[208,128]{1,0:T(8,128)S(1)}, f32[208,128]{1,0:T(8,128)S(1)}, u32[]{:S(2)}, u32[]{:S(2)}) %collective-permute-start.23) | collective-permute-done | bytes 106528 | tf_op jit(solution)/shard_map/ppermute | solution.py:347
  91.7 1.4 %collective-permute-start.24 = (f32[208,128]{1,0:T(8,128)S(1)}, f32[208,128]{1,0:T(8,128)S(1)}, u32[]{:S(2)}, u32[]{:S(2)}) collective-permute-start(f32[208,128]{1,0:T(8,128)S(1)} %add.30), channel_id=1, source_target_pairs={{0,3},{1,2},{2,1},{3,0},{4,7},{5,6},{6,5},{7,4},{8,11},{9,10},{10,... | collective-permute-start | bytes 319496 | tf_op jit(solution)/shard_map/ppermute | solution.py:347
  93.2 1.8 %collective-permute-start.40 = (f32[192,128]{1,0:T(8,128)S(1)}, f32[192,128]{1,0:T(8,128)S(1)}, u32[]{:S(2)}, u32[]{:S(2)}) collective-permute-start(f32[192,128]{1,0:T(8,128)S(1)} %add.34.refs_4_), channel_id=1, source_target_pairs={{0,24},{4,28},{8,16},{12,20},{16,8},{20,12},{24,0},{28,4},{1,25},{... | collective-permute-start | bytes 294920 | tf_op jit(solution)/shard_map/ppermute | solution.py:341
  95.0 0.5 collective-permute-start.38
  95.5 1.3 %collective-permute-start.32 = (f32[192,128]{1,0:T(8,128)S(1)}, f32[192,128]{1,0:T(8,128)S(1)}, u32[]{:S(2)}, u32[]{:S(2)}) collective-permute-start(f32[192,128]{1,0:T(8,128)S(1)} %add.34.refs_4_), channel_id=1, source_target_pairs={{0,16},{4,20},{8,24},{12,28},{16,0},{20,4},{24,8},{28,12},{1,17},{... | collective-permute-start | bytes 294920 | tf_op jit(solution)/shard_map/ppermute | solution.py:341
  96.7 1.6 %collective-permute-done.24 = f32[208,128]{1,0:T(8,128)S(1)} collective-permute-done((f32[208,128]{1,0:T(8,128)S(1)}, f32[208,128]{1,0:T(8,128)S(1)}, u32[]{:S(2)}, u32[]{:S(2)}) %collective-permute-start.24) | collective-permute-done | bytes 106528 | tf_op jit(solution)/shard_map/ppermute | solution.py:347
  98.4 1.8 %collective-permute-start.36 = (f32[208,128]{1,0:T(8,128)S(1)}, f32[208,128]{1,0:T(8,128)S(1)}, u32[]{:S(2)}, u32[]{:S(2)}) collective-permute-start(f32[208,128]{1,0:T(8,128)S(1)} %add.31.refs_0_), channel_id=1, source_target_pairs={{0,24},{4,28},{8,16},{12,20},{16,8},{20,12},{24,0},{28,4},{1,25},{... | collective-permute-start | bytes 319496 | tf_op jit(solution)/shard_map/ppermute | solution.py:341
  100.2 0.6 collective-permute-start.34
  100.8 1.1 %collective-permute-start.26 = (f32[208,128]{1,0:T(8,128)S(1)}, f32[208,128]{1,0:T(8,128)S(1)}, u32[]{:S(2)}, u32[]{:S(2)}) collective-permute-start(f32[208,128]{1,0:T(8,128)S(1)} %add.31.refs_0_), channel_id=1, source_target_pairs={{0,16},{4,20},{8,24},{12,28},{16,0},{20,4},{24,8},{28,12},{1,17},{... | collective-permute-start | bytes 319496 | tf_op jit(solution)/shard_map/ppermute | solution.py:341
  102.0 0.5 collective-permute-start.41
  102.5 1.8 %collective-permute-done.36.refs_10_ = f32[208,128]{1,0:T(8,128)S(1)} collective-permute-done((f32[208,128]{1,0:T(8,128)S(1)}, f32[208,128]{1,0:T(8,128)S(1)}, u32[]{:S(2)}, u32[]{:S(2)}) %collective-permute-start.36) | collective-permute-done | bytes 106528 | tf_op jit(solution)/shard_map/ppermute | solution.py:341
  104.3 0.6 collective-permute-done.34.refs_8_
  104.9 0.6 collective-permute-done.26.refs_2_
  105.5 0.5 collective-permute-start.39
  106.1 0.9 collective-permute-done.39.refs_13_
  107.0 0.4 collective-permute-done.33.refs_7_
  107.5 0.1 copy-done.22
  107.6 0.3 copy-done.23
  108.1 0.6 copy-done.16
  108.7 2.8 %shard_map.127 = (f32[768,512]{1,0:T(8,128)}, f32[3,512]{1,0:T(4,128)}) custom-call(f32[208,128]{1,0:T(8,128)} %copy-done, f32[208,128]{1,0:T(8,128)} %copy-done.13, f32[208,128]{1,0:T(8,128)} %copy-done.12, f32[208,128]{1,0:T(8,128)} %copy-done.16, f32[192,128]{1,0:T(8,128)} %copy-done.1, f32[192,128]{1,0:T(8,128)} %copy-done.20, f32[192,128]{1,0:T(8,128)} %copy-done.19, ...), custom_call_target="tpu_custom_call" | custom-call | bytes 3217408 | tf_op jit(solution)/shard_map/pallas_call | solution.py:31
  (112 shorter events, 0.8 us)
Async XLA Ops:
  0.6 14.2 %collective-permute-start.8 = (bf16[64,768]{1,0:T(8,128)(2,1)}, bf16[64,768]{1,0:T(8,128)(2,1)S(1)}, u32[]{:S(2)}, u32[]{:S(2)}) collective-permute-start(bf16[64,768]{1,0:T(8,128)(2,1)} %refs_0_), channel_id=1, source_target_pairs={{0,16},{4,20},{8,24},{12,28},{16,0},{20,4},{24,8},{28,12},{1,17},{... | collective-permute-start | bytes 294920 | tf_op jit(solution)/shard_map/ppermute | solution.py:341
  3.7 7.2 %collective-permute-start.5 = (bf16[128,768]{1,0:T(8,128)(2,1)}, bf16[128,768]{1,0:T(8,128)(2,1)S(1)}, u32[]{:S(2)}, u32[]{:S(2)}) collective-permute-start(bf16[128,768]{1,0:T(8,128)(2,1)} %refs_4_), channel_id=1, source_target_pairs={{0,16},{4,20},{8,24},{12,28},{16,0},{20,4},{24,8},{28,12},{1,17},{... | collective-permute-start | bytes 589832 | tf_op jit(solution)/shard_map/ppermute | solution.py:341
  7.2 7.8 %collective-permute-start.1 = (bf16[112,512]{1,0:T(8,128)(2,1)}, bf16[112,512]{1,0:T(8,128)(2,1)S(1)}, u32[]{:S(2)}, u32[]{:S(2)}) collective-permute-start(bf16[112,512]{1,0:T(8,128)(2,1)} %get-tuple-element.64.own), channel_id=1, source_target_pairs={{0,1},{1,2},{2,3},{3,0},{4,5},{5,6},{6,7},{7,4},{8,9},{9,10},{10,1... | collective-permute-start | bytes 344072 | tf_op jit(solution)/shard_map/ppermute | solution.py:344
  9.2 13.2 %collective-permute-start.4 = (bf16[128,768]{1,0:T(8,128)(2,1)}, bf16[128,768]{1,0:T(8,128)(2,1)S(1)}, u32[]{:S(2)}, u32[]{:S(2)}) collective-permute-start(bf16[128,768]{1,0:T(8,128)(2,1)} %refs_4_), channel_id=1, source_target_pairs={{0,4},{4,0},{8,12},{12,8},{16,20},{20,16},{24,28},{28,24},{1,5},{5... | collective-permute-start | bytes 589832 | tf_op jit(solution)/shard_map/ppermute | solution.py:341
  10.9 13.8 %copy-start.4 = (bf16[128,768]{1,0:T(8,128)(2,1)}, bf16[128,768]{1,0:T(8,128)(2,1)S(1)}, u32[]{:S(2)}) copy-start(bf16[128,768]{1,0:T(8,128)(2,1)S(1)} %collective-permute-done.5.f_high.refs_6_) | copy-start | bytes 589828
  10.9 11.6 %collective-permute-start.6 = (bf16[128,768]{1,0:T(8,128)(2,1)S(1)}, bf16[128,768]{1,0:T(8,128)(2,1)S(1)}, u32[]{:S(2)}, u32[]{:S(2)}) collective-permute-start(bf16[128,768]{1,0:T(8,128)(2,1)S(1)} %collective-permute-done.5.f_high.refs_6_), channel_id=1, source_target_pairs={{0,4},{4,0},{8,12},{12,8},{16,20},{20,16},{24,28},{28,24},{1,5},{5... | collective-permute-start | bytes 589832 | tf_op jit(solution)/shard_map/ppermute | solution.py:341
  10.9 7.3 %collective-permute-start = (bf16[112,512]{1,0:T(8,128)(2,1)}, bf16[112,512]{1,0:T(8,128)(2,1)S(1)}, u32[]{:S(2)}, u32[]{:S(2)}) collective-permute-start(bf16[112,512]{1,0:T(8,128)(2,1)} %get-tuple-element.64.own), channel_id=1, source_target_pairs={{0,3},{1,0},{2,1},{3,2},{4,7},{5,4},{6,5},{7,6},{8,11},{9,8},{10,9... | collective-permute-start | bytes 344072 | tf_op jit(solution)/shard_map/ppermute | solution.py:344
  14.8 26.4 %copy-start.24 = (bf16[64,768]{1,0:T(8,128)(2,1)}, bf16[64,768]{1,0:T(8,128)(2,1)S(1)}, u32[]{:S(2)}) copy-start(bf16[64,768]{1,0:T(8,128)(2,1)S(1)} %collective-permute-done.8.refs_2_) | copy-start | bytes 294916
  14.8 3.7 %collective-permute-start.7 = (bf16[64,768]{1,0:T(8,128)(2,1)}, bf16[64,768]{1,0:T(8,128)(2,1)S(1)}, u32[]{:S(2)}, u32[]{:S(2)}) collective-permute-start(bf16[64,768]{1,0:T(8,128)(2,1)} %refs_0_), channel_id=1, source_target_pairs={{0,4},{4,0},{8,12},{12,8},{16,20},{20,16},{24,28},{28,24},{1,5},{5... | collective-permute-start | bytes 294920 | tf_op jit(solution)/shard_map/ppermute | solution.py:341
  15.1 9.6 %copy-start.30 = (bf16[112,512]{1,0:T(8,128)(2,1)}, bf16[112,512]{1,0:T(8,128)(2,1)S(1)}, u32[]{:S(2)}) copy-start(bf16[112,512]{1,0:T(8,128)(2,1)S(1)} %collective-permute-done.1.minus) | copy-start | bytes 344068
  15.1 7.4 %collective-permute-start.9 = (bf16[64,768]{1,0:T(8,128)(2,1)S(1)}, bf16[64,768]{1,0:T(8,128)(2,1)S(1)}, u32[]{:S(2)}, u32[]{:S(2)}) collective-permute-start(bf16[64,768]{1,0:T(8,128)(2,1)S(1)} %collective-permute-done.8.refs_2_), channel_id=1, source_target_pairs={{0,4},{4,0},{8,12},{12,8},{16,20},{20,16},{24,28},{28,24},{1,5},{5... | collective-permute-start | bytes 294920 | tf_op jit(solution)/shard_map/ppermute | solution.py:341
  18.2 6.5 %copy-start.31 = (bf16[112,512]{1,0:T(8,128)(2,1)}, bf16[112,512]{1,0:T(8,128)(2,1)S(1)}, u32[]{:S(2)}) copy-start(bf16[112,512]{1,0:T(8,128)(2,1)S(1)} %collective-permute-done.plus) | copy-start | bytes 344068
  18.2 6.4 %collective-permute-start.3 = (bf16[56,512]{1,0:T(8,128)(2,1)S(1)}, bf16[56,512]{1,0:T(8,128)(2,1)S(1)}, u32[]{:S(2)}, u32[]{:S(2)}) collective-permute-start(bf16[56,512]{1,0:T(8,128)(2,1)S(1)} %slice.17), channel_id=1, source_target_pairs={{0,1},{1,2},{2,3},{3,0},{4,5},{5,6},{6,7},{7,4},{8,9},{9,10},{10,1... | collective-permute-start | bytes 172040 | tf_op jit(solution)/shard_map/ppermute | solution.py:344
  18.6 22.6 %copy-start.25 = (bf16[64,768]{1,0:T(8,128)(2,1)}, bf16[64,768]{1,0:T(8,128)(2,1)S(1)}, u32[]{:S(2)}) copy-start(bf16[64,768]{1,0:T(8,128)(2,1)S(1)} %collective-permute-done.7.refs_1_) | copy-start | bytes 294916
  18.6 6.1 %collective-permute-start.2 = (bf16[56,512]{1,0:T(8,128)(2,1)S(1)}, bf16[56,512]{1,0:T(8,128)(2,1)S(1)}, u32[]{:S(2)}, u32[]{:S(2)}) collective-permute-start(bf16[56,512]{1,0:T(8,128)(2,1)S(1)} %slice.16), channel_id=1, source_target_pairs={{0,3},{1,0},{2,1},{3,2},{4,7},{5,4},{6,5},{7,6},{8,11},{9,8},{10,9... | collective-permute-start | bytes 172040 | tf_op jit(solution)/shard_map/ppermute | solution.py:344
  22.5 18.7 %copy-start.26 = (bf16[64,768]{1,0:T(8,128)(2,1)}, bf16[64,768]{1,0:T(8,128)(2,1)S(1)}, u32[]{:S(2)}) copy-start(bf16[64,768]{1,0:T(8,128)(2,1)S(1)} %collective-permute-done.9.refs_3_) | copy-start | bytes 294916
  22.5 2.2 %copy-start.5 = (bf16[128,768]{1,0:T(8,128)(2,1)}, bf16[128,768]{1,0:T(8,128)(2,1)S(1)}, u32[]{:S(2)}) copy-start(bf16[128,768]{1,0:T(8,128)(2,1)S(1)} %collective-permute-done.4.f_low.refs_5_) | copy-start | bytes 589828
  22.5 2.2 %copy-start.6 = (bf16[128,768]{1,0:T(8,128)(2,1)}, bf16[128,768]{1,0:T(8,128)(2,1)S(1)}, u32[]{:S(2)}) copy-start(bf16[128,768]{1,0:T(8,128)(2,1)S(1)} %collective-permute-done.6.f_far.refs_7_) | copy-start | bytes 589828
  41.2 1.8 %collective-permute-start.14 = (f32[528,128]{1,0:T(8,128)}, f32[528,128]{1,0:T(8,128)S(1)}, u32[]{:S(2)}, u32[]{:S(2)}) collective-permute-start(f32[528,128]{1,0:T(8,128)} %get-tuple-element.96), channel_id=1, source_target_pairs={{0,4},{4,0},{8,12},{12,8},{16,20},{20,16},{24,28},{28,24},{1,5},{5... | collective-permute-start | bytes 811016 | tf_op jit(solution)/shard_map/ppermute | solution.py:341
  41.3 8.6 %collective-permute-start.13 = (f32[528,128]{1,0:T(8,128)}, f32[528,128]{1,0:T(8,128)S(1)}, u32[]{:S(2)}, u32[]{:S(2)}) collective-permute-start(f32[528,128]{1,0:T(8,128)} %get-tuple-element.77), channel_id=1, source_target_pairs={{0,4},{4,0},{8,12},{12,8},{16,20},{20,16},{24,28},{28,24},{1,5},{5... | collective-permute-start | bytes 811016 | tf_op jit(solution)/shard_map/ppermute | solution.py:341
  44.0 18.1 %collective-permute-start.15 = (f32[528,128]{1,0:T(8,128)S(1)}, f32[528,128]{1,0:T(8,128)S(1)}, u32[]{:S(2)}, u32[]{:S(2)}) collective-permute-start(f32[528,128]{1,0:T(8,128)S(1)} %add.28), channel_id=1, source_target_pairs={{0,16},{4,20},{8,24},{12,28},{16,0},{20,4},{24,8},{28,12},{1,17},{... | collective-permute-start | bytes 811016 | tf_op jit(solution)/shard_map/ppermute | solution.py:341
  45.5 7.5 %collective-permute-start.10 = (f32[64,512]{1,0:T(8,128)}, f32[64,512]{1,0:T(8,128)S(1)}, u32[]{:S(2)}, u32[]{:S(2)}) collective-permute-start(f32[64,512]{1,0:T(8,128)} %get-tuple-element.70), channel_id=1, source_target_pairs={{0,1},{1,0},{2,3},{3,2},{4,5},{5,4},{6,7},{7,6},{8,9},{9,8},{10,11... | collective-permute-start | bytes 393224 | tf_op jit(solution)/shard_map/ppermute | solution.py:347
  46.2 13.3 %collective-permute-start.11 = (f32[64,512]{1,0:T(8,128)}, f32[64,512]{1,0:T(8,128)S(1)}, u32[]{:S(2)}, u32[]{:S(2)}) collective-permute-start(f32[64,512]{1,0:T(8,128)} %get-tuple-element.71), channel_id=1, source_target_pairs={{0,2},{1,3},{2,0},{3,1},{4,6},{5,7},{6,4},{7,5},{8,10},{9,11},{10,... | collective-permute-start | bytes 393224 | tf_op jit(solution)/shard_map/ppermute | solution.py:347
  49.3 10.2 %collective-permute-start.12 = (f32[64,512]{1,0:T(8,128)}, f32[64,512]{1,0:T(8,128)S(1)}, u32[]{:S(2)}, u32[]{:S(2)}) collective-permute-start(f32[64,512]{1,0:T(8,128)} %get-tuple-element.72), channel_id=1, source_target_pairs={{0,3},{1,2},{2,1},{3,0},{4,7},{5,6},{6,5},{7,4},{8,11},{9,10},{10,... | collective-permute-start | bytes 393224 | tf_op jit(solution)/shard_map/ppermute | solution.py:347
  49.9 14.1 %copy-start.2 = (f32[528,128]{1,0:T(8,128)}, f32[528,128]{1,0:T(8,128)S(1)}, u32[]{:S(2)}) copy-start(f32[528,128]{1,0:T(8,128)S(1)} %collective-permute-done.13.recv) | copy-start | bytes 811012
  53.0 6.5 %copy-start.7 = (f32[64,512]{1,0:T(8,128)}, f32[64,512]{1,0:T(8,128)S(1)}, u32[]{:S(2)}) copy-start(f32[64,512]{1,0:T(8,128)S(1)} %collective-permute-done.10.b) | copy-start | bytes 393220
  62.1 4.9 %collective-permute-start.19 = (bf16[64,128]{1,0:T(8,128)(2,1)}, bf16[64,128]{1,0:T(8,128)(2,1)S(1)}, u32[]{:S(2)}, u32[]{:S(2)}) collective-permute-start(bf16[64,128]{1,0:T(8,128)(2,1)} %get-tuple-element.108), channel_id=1, source_target_pairs={{0,4},{4,0},{8,12},{12,8},{16,20},{20,16},{24,28},{28,24},{1,5},{5... | collective-permute-start | bytes 49160 | tf_op jit(solution)/shard_map/ppermute | solution.py:341
  62.2 4.8 %collective-permute-start.20 = (bf16[64,128]{1,0:T(8,128)(2,1)}, bf16[64,128]{1,0:T(8,128)(2,1)S(1)}, u32[]{:S(2)}, u32[]{:S(2)}) collective-permute-start(bf16[64,128]{1,0:T(8,128)(2,1)} %get-tuple-element.109), channel_id=1, source_target_pairs={{0,16},{4,20},{8,24},{12,28},{16,0},{20,4},{24,8},{28,12},{1,17},{... | collective-permute-start | bytes 49160 | tf_op jit(solution)/shard_map/ppermute | solution.py:341
  62.9 4.1 %collective-permute-start.21 = (bf16[64,128]{1,0:T(8,128)(2,1)}, bf16[64,128]{1,0:T(8,128)(2,1)S(1)}, u32[]{:S(2)}, u32[]{:S(2)}) collective-permute-start(bf16[64,128]{1,0:T(8,128)(2,1)} %get-tuple-element.110), channel_id=1, source_target_pairs={{0,20},{4,16},{8,28},{12,24},{16,4},{20,0},{24,12},{28,8},{1,21},{... | collective-permute-start | bytes 49160 | tf_op jit(solution)/shard_map/ppermute | solution.py:341
  69.8 5.9 %collective-permute-start.28 = (f32[192,128]{1,0:T(8,128)}, f32[192,128]{1,0:T(8,128)S(1)}, u32[]{:S(2)}, u32[]{:S(2)}) collective-permute-start(f32[192,128]{1,0:T(8,128)} %get-tuple-element.121), channel_id=1, source_target_pairs={{0,8},{4,12},{8,0},{12,4},{16,24},{20,28},{24,16},{28,20},{1,9},{5... | collective-permute-start | bytes 294920 | tf_op jit(solution)/shard_map/ppermute | solution.py:341
  71.3 13.6 %collective-permute-start.22 = (f32[208,128]{1,0:T(8,128)}, f32[208,128]{1,0:T(8,128)S(1)}, u32[]{:S(2)}, u32[]{:S(2)}) collective-permute-start(f32[208,128]{1,0:T(8,128)} %get-tuple-element.111), channel_id=1, source_target_pairs={{0,8},{4,12},{8,0},{12,4},{16,24},{20,28},{24,16},{28,20},{1,9},{5... | collective-permute-start | bytes 319496 | tf_op jit(solution)/shard_map/ppermute | solution.py:341
  76.6 10.4 %collective-permute-start.29 = (f32[192,128]{1,0:T(8,128)S(1)}, f32[192,128]{1,0:T(8,128)S(1)}, u32[]{:S(2)}, u32[]{:S(2)}) collective-permute-start(f32[192,128]{1,0:T(8,128)S(1)} %add.32), channel_id=1, source_target_pairs={{0,3},{1,2},{2,1},{3,0},{4,7},{5,6},{6,5},{7,4},{8,11},{9,10},{10,... | collective-permute-start | bytes 294920 | tf_op jit(solution)/shard_map/ppermute | solution.py:347
  79.2 1.9 %collective-permute-start.16 = (f32[128,128]{1,0:T(8,128)}, f32[128,128]{1,0:T(8,128)S(1)}, u32[]{:S(2)}, u32[]{:S(2)}) collective-permute-start(f32[128,128]{1,0:T(8,128)} %get-tuple-element.101), channel_id=1, source_target_pairs={{0,4},{4,0},{8,12},{12,8},{16,20},{20,16},{24,28},{28,24},{1,5},{5... | collective-permute-start | bytes 196616 | tf_op jit(solution)/shard_map/ppermute | solution.py:341
  79.2 5.2 %collective-permute-start.17 = (f32[128,128]{1,0:T(8,128)}, f32[128,128]{1,0:T(8,128)S(1)}, u32[]{:S(2)}, u32[]{:S(2)}) collective-permute-start(f32[128,128]{1,0:T(8,128)} %get-tuple-element.102), channel_id=1, source_target_pairs={{0,16},{4,20},{8,24},{12,28},{16,0},{20,4},{24,8},{28,12},{1,17},{... | collective-permute-start | bytes 196616 | tf_op jit(solution)/shard_map/ppermute | solution.py:341
  79.9 5.0 %collective-permute-start.18 = (f32[128,128]{1,0:T(8,128)}, f32[128,128]{1,0:T(8,128)S(1)}, u32[]{:S(2)}, u32[]{:S(2)}) collective-permute-start(f32[128,128]{1,0:T(8,128)} %get-tuple-element.103), channel_id=1, source_target_pairs={{0,20},{4,16},{8,28},{12,24},{16,4},{20,0},{24,12},{28,8},{1,21},{... | collective-permute-start | bytes 196616 | tf_op jit(solution)/shard_map/ppermute | solution.py:341
  81.1 6.9 %copy-start.27 = (f32[128,128]{1,0:T(8,128)}, f32[128,128]{1,0:T(8,128)S(1)}, u32[]{:S(2)}) copy-start(f32[128,128]{1,0:T(8,128)S(1)} %collective-permute-done.16.refs_1_) | copy-start | bytes 196612
  84.4 3.6 %copy-start.28 = (f32[128,128]{1,0:T(8,128)}, f32[128,128]{1,0:T(8,128)S(1)}, u32[]{:S(2)}) copy-start(f32[128,128]{1,0:T(8,128)S(1)} %collective-permute-done.17.refs_2_) | copy-start | bytes 196612
  84.9 3.1 %copy-start.29 = (f32[128,128]{1,0:T(8,128)}, f32[128,128]{1,0:T(8,128)S(1)}, u32[]{:S(2)}) copy-start(f32[128,128]{1,0:T(8,128)S(1)} %collective-permute-done.18.refs_3_) | copy-start | bytes 196612
  85.8 5.9 %collective-permute-start.23 = (f32[208,128]{1,0:T(8,128)S(1)}, f32[208,128]{1,0:T(8,128)S(1)}, u32[]{:S(2)}, u32[]{:S(2)}) collective-permute-start(f32[208,128]{1,0:T(8,128)S(1)} %add.29), channel_id=1, source_target_pairs={{0,1},{1,0},{2,3},{3,2},{4,5},{5,4},{6,7},{7,6},{8,9},{9,8},{10,11... | collective-permute-start | bytes 319496 | tf_op jit(solution)/shard_map/ppermute | solution.py:347
  87.1 6.1 %collective-permute-start.30 = (f32[192,128]{1,0:T(8,128)S(1)}, f32[192,128]{1,0:T(8,128)S(1)}, u32[]{:S(2)}, u32[]{:S(2)}) collective-permute-start(f32[192,128]{1,0:T(8,128)S(1)} %add.33), channel_id=1, source_target_pairs={{0,1},{1,0},{2,3},{3,2},{4,5},{5,4},{6,7},{7,6},{8,9},{9,8},{10,11... | collective-permute-start | bytes 294920 | tf_op jit(solution)/shard_map/ppermute | solution.py:347
  91.7 6.6 %collective-permute-start.24 = (f32[208,128]{1,0:T(8,128)S(1)}, f32[208,128]{1,0:T(8,128)S(1)}, u32[]{:S(2)}, u32[]{:S(2)}) collective-permute-start(f32[208,128]{1,0:T(8,128)S(1)} %add.30), channel_id=1, source_target_pairs={{0,3},{1,2},{2,1},{3,0},{4,7},{5,6},{6,5},{7,4},{8,11},{9,10},{10,... | collective-permute-start | bytes 319496 | tf_op jit(solution)/shard_map/ppermute | solution.py:347
  93.2 14.2 %copy-start.1 = (f32[192,128]{1,0:T(8,128)}, f32[192,128]{1,0:T(8,128)S(1)}, u32[]{:S(2)}) copy-start(f32[192,128]{1,0:T(8,128)S(1)} %add.34.refs_4_) | copy-start | bytes 294916
  93.2 7.0 %collective-permute-start.40 = (f32[192,128]{1,0:T(8,128)S(1)}, f32[192,128]{1,0:T(8,128)S(1)}, u32[]{:S(2)}, u32[]{:S(2)}) collective-permute-start(f32[192,128]{1,0:T(8,128)S(1)} %add.34.refs_4_), channel_id=1, source_target_pairs={{0,24},{4,28},{8,16},{12,20},{16,8},{20,12},{24,0},{28,4},{1,25},{... | collective-permute-start | bytes 294920 | tf_op jit(solution)/shard_map/ppermute | solution.py:341
  95.0 5.9 %collective-permute-start.38 = (f32[192,128]{1,0:T(8,128)S(1)}, f32[192,128]{1,0:T(8,128)S(1)}, u32[]{:S(2)}, u32[]{:S(2)}) collective-permute-start(f32[192,128]{1,0:T(8,128)S(1)} %add.34.refs_4_), channel_id=1, source_target_pairs={{0,8},{4,12},{8,0},{12,4},{16,24},{20,28},{24,16},{28,20},{1,9},{5... | collective-permute-start | bytes 294920 | tf_op jit(solution)/shard_map/ppermute | solution.py:341
  95.5 6.5 %collective-permute-start.32 = (f32[192,128]{1,0:T(8,128)S(1)}, f32[192,128]{1,0:T(8,128)S(1)}, u32[]{:S(2)}, u32[]{:S(2)}) collective-permute-start(f32[192,128]{1,0:T(8,128)S(1)} %add.34.refs_4_), channel_id=1, source_target_pairs={{0,16},{4,20},{8,24},{12,28},{16,0},{20,4},{24,8},{28,12},{1,17},{... | collective-permute-start | bytes 294920 | tf_op jit(solution)/shard_map/ppermute | solution.py:341
  96.7 5.2 %collective-permute-start.31 = (f32[192,128]{1,0:T(8,128)S(1)}, f32[192,128]{1,0:T(8,128)S(1)}, u32[]{:S(2)}, u32[]{:S(2)}) collective-permute-start(f32[192,128]{1,0:T(8,128)S(1)} %add.34.refs_4_), channel_id=1, source_target_pairs={{0,4},{4,0},{8,12},{12,8},{16,20},{20,16},{24,28},{28,24},{1,5},{5... | collective-permute-start | bytes 294920 | tf_op jit(solution)/shard_map/ppermute | solution.py:341
  98.4 9.0 %copy-start = (f32[208,128]{1,0:T(8,128)}, f32[208,128]{1,0:T(8,128)S(1)}, u32[]{:S(2)}) copy-start(f32[208,128]{1,0:T(8,128)S(1)} %add.31.refs_0_) | copy-start | bytes 319492
  98.4 5.9 %collective-permute-start.36 = (f32[208,128]{1,0:T(8,128)S(1)}, f32[208,128]{1,0:T(8,128)S(1)}, u32[]{:S(2)}, u32[]{:S(2)}) collective-permute-start(f32[208,128]{1,0:T(8,128)S(1)} %add.31.refs_0_), channel_id=1, source_target_pairs={{0,24},{4,28},{8,16},{12,20},{16,8},{20,12},{24,0},{28,4},{1,25},{... | collective-permute-start | bytes 319496 | tf_op jit(solution)/shard_map/ppermute | solution.py:341
  100.2 7.2 %copy-start.17 = (f32[192,128]{1,0:T(8,128)}, f32[192,128]{1,0:T(8,128)S(1)}, u32[]{:S(2)}) copy-start(f32[192,128]{1,0:T(8,128)S(1)} %collective-permute-done.40.refs_14_) | copy-start | bytes 294916
  100.2 4.7 %collective-permute-start.34 = (f32[208,128]{1,0:T(8,128)S(1)}, f32[208,128]{1,0:T(8,128)S(1)}, u32[]{:S(2)}, u32[]{:S(2)}) collective-permute-start(f32[208,128]{1,0:T(8,128)S(1)} %add.31.refs_0_), channel_id=1, source_target_pairs={{0,8},{4,12},{8,0},{12,4},{16,24},{20,28},{24,16},{28,20},{1,9},{5... | collective-permute-start | bytes 319496 | tf_op jit(solution)/shard_map/ppermute | solution.py:341
  100.8 6.6 %copy-start.18 = (f32[192,128]{1,0:T(8,128)}, f32[192,128]{1,0:T(8,128)S(1)}, u32[]{:S(2)}) copy-start(f32[192,128]{1,0:T(8,128)S(1)} %collective-permute-done.38.refs_12_) | copy-start | bytes 294916
  100.8 4.7 %collective-permute-start.26 = (f32[208,128]{1,0:T(8,128)S(1)}, f32[208,128]{1,0:T(8,128)S(1)}, u32[]{:S(2)}, u32[]{:S(2)}) collective-permute-start(f32[208,128]{1,0:T(8,128)S(1)} %add.31.refs_0_), channel_id=1, source_target_pairs={{0,16},{4,20},{8,24},{12,28},{16,0},{20,4},{24,8},{28,12},{1,17},{... | collective-permute-start | bytes 319496 | tf_op jit(solution)/shard_map/ppermute | solution.py:341
  102.0 5.5 %copy-start.19 = (f32[192,128]{1,0:T(8,128)}, f32[192,128]{1,0:T(8,128)S(1)}, u32[]{:S(2)}) copy-start(f32[192,128]{1,0:T(8,128)S(1)} %collective-permute-done.32.refs_6_) | copy-start | bytes 294916
  102.0 3.6 %collective-permute-start.25 = (f32[208,128]{1,0:T(8,128)S(1)}, f32[208,128]{1,0:T(8,128)S(1)}, u32[]{:S(2)}, u32[]{:S(2)}) collective-permute-start(f32[208,128]{1,0:T(8,128)S(1)} %add.31.refs_0_), channel_id=1, source_target_pairs={{0,4},{4,0},{8,12},{12,8},{16,20},{20,16},{24,28},{28,24},{1,5},{5... | collective-permute-start | bytes 319496 | tf_op jit(solution)/shard_map/ppermute | solution.py:341
  102.0 5.5 %copy-start.20 = (f32[192,128]{1,0:T(8,128)}, f32[192,128]{1,0:T(8,128)S(1)}, u32[]{:S(2)}) copy-start(f32[192,128]{1,0:T(8,128)S(1)} %collective-permute-done.31.refs_5_) | copy-start | bytes 294916
  102.0 4.1 %collective-permute-start.41 = (f32[192,128]{1,0:T(8,128)S(1)}, f32[192,128]{1,0:T(8,128)S(1)}, u32[]{:S(2)}, u32[]{:S(2)}) collective-permute-start(f32[192,128]{1,0:T(8,128)S(1)} %collective-permute-done.40.refs_14_), channel_id=1, source_target_pairs={{0,4},{4,0},{8,12},{12,8},{16,20},{20,16},{24,28},{28,24},{1,5},{5... | collective-permute-start | bytes 294920 | tf_op jit(solution)/shard_map/ppermute | solution.py:341
  104.3 3.1 %copy-start.10 = (f32[208,128]{1,0:T(8,128)}, f32[208,128]{1,0:T(8,128)S(1)}, u32[]{:S(2)}) copy-start(f32[208,128]{1,0:T(8,128)S(1)} %collective-permute-done.36.refs_10_) | copy-start | bytes 319492
  104.3 3.0 %collective-permute-start.37 = (f32[208,128]{1,0:T(8,128)S(1)}, f32[208,128]{1,0:T(8,128)S(1)}, u32[]{:S(2)}, u32[]{:S(2)}) collective-permute-start(f32[208,128]{1,0:T(8,128)S(1)} %collective-permute-done.36.refs_10_), channel_id=1, source_target_pairs={{0,4},{4,0},{8,12},{12,8},{16,20},{20,16},{24,28},{28,24},{1,5},{5... | collective-permute-start | bytes 319496 | tf_op jit(solution)/shard_map/ppermute | solution.py:341
  104.9 2.6 %copy-start.11 = (f32[208,128]{1,0:T(8,128)}, f32[208,128]{1,0:T(8,128)S(1)}, u32[]{:S(2)}) copy-start(f32[208,128]{1,0:T(8,128)S(1)} %collective-permute-done.34.refs_8_) | copy-start | bytes 319492
  104.9 2.5 %collective-permute-start.35 = (f32[208,128]{1,0:T(8,128)S(1)}, f32[208,128]{1,0:T(8,128)S(1)}, u32[]{:S(2)}, u32[]{:S(2)}) collective-permute-start(f32[208,128]{1,0:T(8,128)S(1)} %collective-permute-done.34.refs_8_), channel_id=1, source_target_pairs={{0,4},{4,0},{8,12},{12,8},{16,20},{20,16},{24,28},{28,24},{1,5},{5... | collective-permute-start | bytes 319496 | tf_op jit(solution)/shard_map/ppermute | solution.py:341
  105.5 1.9 %copy-start.12 = (f32[208,128]{1,0:T(8,128)}, f32[208,128]{1,0:T(8,128)S(1)}, u32[]{:S(2)}) copy-start(f32[208,128]{1,0:T(8,128)S(1)} %collective-permute-done.26.refs_2_) | copy-start | bytes 319492
  105.5 1.9 %collective-permute-start.27 = (f32[208,128]{1,0:T(8,128)S(1)}, f32[208,128]{1,0:T(8,128)S(1)}, u32[]{:S(2)}, u32[]{:S(2)}) collective-permute-start(f32[208,128]{1,0:T(8,128)S(1)} %collective-permute-done.26.refs_2_), channel_id=1, source_target_pairs={{0,4},{4,0},{8,12},{12,8},{16,20},{20,16},{24,28},{28,24},{1,5},{5... | collective-permute-start | bytes 319496 | tf_op jit(solution)/shard_map/ppermute | solution.py:341
  105.5 1.4 %collective-permute-start.39 = (f32[192,128]{1,0:T(8,128)S(1)}, f32[192,128]{1,0:T(8,128)S(1)}, u32[]{:S(2)}, u32[]{:S(2)}) collective-permute-start(f32[192,128]{1,0:T(8,128)S(1)} %collective-permute-done.38.refs_12_), channel_id=1, source_target_pairs={{0,4},{4,0},{8,12},{12,8},{16,20},{20,16},{24,28},{28,24},{1,5},{5... | collective-permute-start | bytes 294920 | tf_op jit(solution)/shard_map/ppermute | solution.py:341
  106.0 1.3 %collective-permute-start.33 = (f32[192,128]{1,0:T(8,128)S(1)}, f32[192,128]{1,0:T(8,128)S(1)}, u32[]{:S(2)}, u32[]{:S(2)}) collective-permute-start(f32[192,128]{1,0:T(8,128)S(1)} %collective-permute-done.32.refs_6_), channel_id=1, source_target_pairs={{0,4},{4,0},{8,12},{12,8},{16,20},{20,16},{24,28},{28,24},{1,5},{5... | collective-permute-start | bytes 294920 | tf_op jit(solution)/shard_map/ppermute | solution.py:341
  (15 other events, 13.0 us)
where the time goes:
time: 112 us
  starting transfers between devices  40.3 us (36%)
  Pallas kernels  32.1 us (29%)
  waiting for transfers between devices  30 us (27%)
  other arithmetic  4.22 us (4%)
  local copies, waits for them, and re-layouts  3.82 us (3%)
    pallas_call x8, Pallas kernels, call(): pl.pallas_call(body, out_shape=tuple(outs), in_specs=in_specs or [VMEM] *...  32.1 us
    ppermute x31, starting transfers between devices, met(): return lax.ppermute(x, 'bucket', [(i, i ^ mask) for i in range(buckets)])  19.7 us
    ppermute x31, waiting for transfers between devices, met(): return lax.ppermute(x, 'bucket', [(i, i ^ mask) for i in range(buckets)])  14.9 us
    ppermute x7, starting transfers between devices, crossed(): return lax.ppermute(x, 'rel', [(i, i ^ mask) for i in range(groups)])  10.5 us
    ppermute x7, waiting for transfers between devices, crossed(): return lax.ppermute(x, 'rel', [(i, i ^ mask) for i in range(groups)])  10.2 us
    ppermute x4, starting transfers between devices, ring(): lax.ppermute(x, 'rel', [(i, (i - step) % groups) for i in range(groups)])  10.1 us
    ppermute x4, waiting for transfers between devices, ring(): lax.ppermute(x, 'rel', [(i, (i - step) % groups) for i in range(groups)])  5.01 us
    unnamed x74, local copies, waits for them, and re-layouts  3.81 us
  transfers between devices with their start and end apart: 42, of which 15 were waited for; matrix products, arithmetic and copies ran while one was open for 4% of the time, Pallas kernels for 11%

commit v1 on v0

--- a/solution.py
+++ b/solution.py
@@ -134,13 +134,23 @@
 
 
 def prepare_body(size, *refs):
-    src, tgt, weight, (act, src_turned, tgt_turned, src_held, tgt_held) = refs[:4], refs[4:8], refs[8], refs[9:]
-    me = own_quarter(size)
-    for feats, held, turned in ((src, src_held, src_turned), (tgt, tgt_held, tgt_turned)):
-        for j, x in enumerate(feats):
-            held[aligned(me ^ APART[j], x.shape[0]), :] = x[...]
+    src, tgt, weight, (act, src_turned, tgt_turned, src_held, tgt_held, columns, sems) = refs[:4], refs[4:8], refs[8], refs[9:]
+    me = own_quarter(size)
+    copies = [(weight.at[:, aligned(me, act.shape[1])], columns)]
+    for feats, held in ((src, src_held), (tgt, tgt_held)):
+        copies += [(x, held.at[aligned(me ^ APART[j], x.shape[0])]) for j, x in enumerate(feats)]
+    start_all(copies, sems)
+    for held, turned in ((src_held, src_turned), (tgt_held, tgt_turned)):
         turned[...] = held[...].astype(F32).T.astype(BF16)
-    act[...] = jnp.tanh(dot(tgt_held[...], weight[:, aligned(me, act.shape[1])], NN))
+    act[...] = jnp.tanh(dot(tgt_held[...], columns[...], NN))
+
+
+def start_all(copies, sems):
+    started = [pltpu.make_async_copy(a, b, sems.at[i]) for i, (a, b) in enumerate(copies)]
+    for c in started:
+        c.start()
+    for c in started:
+        c.wait()
 
 
 def spread(pieces, targets):
@@ -403,7 +413,13 @@
         functools.partial(prepare_body, buckets),
         [shaped((4 * t_rows, wide)), shaped((feat, 4 * s_rows), BF16), shaped((feat, 4 * t_rows), BF16)],
         [*s_feats, *t_feats, enc_weight],
-        scratch=[pltpu.VMEM((4 * s_rows, feat), BF16), pltpu.VMEM((4 * t_rows, feat), BF16)],
+        in_specs=[ANY] * 9,
+        scratch=[
+            pltpu.VMEM((4 * s_rows, feat), BF16),
+            pltpu.VMEM((4 * t_rows, feat), BF16),
+            pltpu.VMEM((feat, wide), BF16),
+            pltpu.SemaphoreType.DMA((9,)),
+        ],
         flops=8 * t_rows * feat * wide,
     )
     s_parts, act = lax.optimization_barrier((s_parts, act))

time: 112 us -> 112 us (level)
  transfers between devices with their start and end apart: 42 -> 42, of which waited for: 15 -> 16; matrix products, arithmetic and copies ran while one was open for 4% -> 4% of each run, Pallas kernels for 11% -> 10%
where the time goes in v1:
time: 112 us
  starting transfers between devices  40.3 us (36%)
  Pallas kernels  31.9 us (28%)
  waiting for transfers between devices  30.2 us (27%)
  other arithmetic  4.22 us (4%)
  local copies, waits for them, and re-layouts  3.82 us (3%)
    pallas_call x8, Pallas kernels, call(): pl.pallas_call(body, out_shape=tuple(outs), in_specs=in_specs or [VMEM] *...  31.9 us
    ppermute x31, starting transfers between devices, met(): return lax.ppermute(x, 'bucket', [(i, i ^ mask) for i in range(buckets)])  19.7 us
    ppermute x31, waiting for transfers between devices, met(): return lax.ppermute(x, 'bucket', [(i, i ^ mask) for i in range(buckets)])  14.9 us
    ppermute x7, starting transfers between devices, crossed(): return lax.ppermute(x, 'rel', [(i, i ^ mask) for i in range(groups)])  10.5 us
    ppermute x7, waiting for transfers between devices, crossed(): return lax.ppermute(x, 'rel', [(i, i ^ mask) for i in range(groups)])  10.4 us
    ppermute x4, starting transfers between devices, ring(): lax.ppermute(x, 'rel', [(i, (i - step) % groups) for i in range(groups)])  10.1 us
    ppermute x4, waiting for transfers between devices, ring(): lax.ppermute(x, 'rel', [(i, (i - step) % groups) for i in range(groups)])  5.01 us
    unnamed x74, local copies, waits for them, and re-layouts  3.81 us
  transfers between devices with their start and end apart: 42, of which 16 were waited for; matrix products, arithmetic and copies ran while one was open for 4% of the time, Pallas kernels for 10%

profile of v1, /device:TPU:0, one launch (start us, length us, event | category | flops | bytes accessed | tf_op | source)
XLA Modules:
  0.0 111.6 jit_solution(16190664545503774401)
XLA Ops:
  0.6 3.1 %collective-permute-start.8 = (bf16[64,768]{1,0:T(8,128)(2,1)}, bf16[64,768]{1,0:T(8,128)(2,1)S(1)}, u32[]{:S(2)}, u32[]{:S(2)}) collective-permute-start(bf16[64,768]{1,0:T(8,128)(2,1)} %refs_0_), channel_id=1, source_target_pairs={{0,16},{4,20},{8,24},{12,28},{16,0},{20,4},{24,8},{28,12},{1,17},{... | collective-permute-start | bytes 294920 | tf_op jit(solution)/shard_map/ppermute | solution.py:351
  3.8 1.3 %add_bitcast_fusion.rel = s32[4,768]{1,0:T(4,128)} fusion(s32[1,1,4,3,768]{4,2,3,1,0:T(4,128)} %param.15), kind=kLoop, calls=%fused_computation | loop fusion | flops 6144 | bytes 36864 | tf_op jit(solution)/shard_map/add | solution.py:367
  5.1 2.1 %shard_map.120 = (bf16[112,512]{1,0:T(8,128)(2,1)}, f32[64,512]{1,0:T(8,128)}) custom-call(bf16[64,768]{1,0:T(8,128)(2,1)} %refs_0_, bf16[768,512]{1,0:T(8,128)(2,1)} %refs_8_.1, s32[1,1,4,768]{3,2,1,0:T(4,128)} %src.1, s32[1,1,4,768]{3,2,1,0:T(4,128)} %tgt.1, s32[4,768]{1,0:T(4,128)} %add_bitcast_fusion.rel, s32[1,1,4,128]{3,2,1,0:T(4,128)} %neg.1, ...), custom_call_target="tpu_custom_call" | custom-call | flops 50331648 | bytes 1184768 | tf_op jit(solution)/shard_map/pallas_call | solution.py:31
  7.2 2.0 %collective-permute-start.1 = (bf16[112,512]{1,0:T(8,128)(2,1)}, bf16[112,512]{1,0:T(8,128)(2,1)S(1)}, u32[]{:S(2)}, u32[]{:S(2)}) collective-permute-start(bf16[112,512]{1,0:T(8,128)(2,1)} %get-tuple-element.64.own), channel_id=1, source_target_pairs={{0,1},{1,2},{2,3},{3,0},{4,5},{5,6},{6,7},{7,4},{8,9},{9,10},{10,1... | collective-permute-start | bytes 344072 | tf_op jit(solution)/shard_map/ppermute | solution.py:354
  9.2 1.7 %collective-permute-done.5.f_high.refs_6_ = bf16[128,768]{1,0:T(8,128)(2,1)S(1)} collective-permute-done((bf16[128,768]{1,0:T(8,128)(2,1)}, bf16[128,768]{1,0:T(8,128)(2,1)S(1)}, u32[]{:S(2)}, u32[]{:S(2)}) %collective-permute-start.5) | collective-permute-done | bytes 196640 | tf_op jit(solution)/shard_map/ppermute | solution.py:351
  10.9 3.9 %collective-permute-start = (bf16[112,512]{1,0:T(8,128)(2,1)}, bf16[112,512]{1,0:T(8,128)(2,1)S(1)}, u32[]{:S(2)}, u32[]{:S(2)}) collective-permute-start(bf16[112,512]{1,0:T(8,128)(2,1)} %get-tuple-element.64.own), channel_id=1, source_target_pairs={{0,3},{1,0},{2,1},{3,2},{4,7},{5,4},{6,5},{7,6},{8,11},{9,8},{10,9... | collective-permute-start | bytes 344072 | tf_op jit(solution)/shard_map/ppermute | solution.py:354
  14.8 0.2 collective-permute-start.7
  15.1 0.3 collective-permute-start.9
  15.3 2.9 %collective-permute-done.plus = bf16[112,512]{1,0:T(8,128)(2,1)S(1)} collective-permute-done((bf16[112,512]{1,0:T(8,128)(2,1)}, bf16[112,512]{1,0:T(8,128)(2,1)S(1)}, u32[]{:S(2)}, u32[]{:S(2)}) %collective-permute-start) | collective-permute-done | bytes 114720 | tf_op jit(solution)/shard_map/ppermute | solution.py:354
  18.2 0.4 collective-permute-start.3
  18.6 3.9 %collective-permute-start.2 = (bf16[56,512]{1,0:T(8,128)(2,1)S(1)}, bf16[56,512]{1,0:T(8,128)(2,1)S(1)}, u32[]{:S(2)}, u32[]{:S(2)}) collective-permute-start(bf16[56,512]{1,0:T(8,128)(2,1)S(1)} %slice.16), channel_id=1, source_target_pairs={{0,3},{1,0},{2,1},{3,2},{4,7},{5,4},{6,5},{7,6},{8,11},{9,8},{10,9... | collective-permute-start | bytes 172040 | tf_op jit(solution)/shard_map/ppermute | solution.py:354
  22.5 2.1 %collective-permute-done.3.far_b = bf16[56,512]{1,0:T(8,128)(2,1)S(1)} collective-permute-done((bf16[56,512]{1,0:T(8,128)(2,1)S(1)}, bf16[56,512]{1,0:T(8,128)(2,1)S(1)}, u32[]{:S(2)}, u32[]{:S(2)}) %collective-permute-start.3) | collective-permute-done | bytes 57376 | tf_op jit(solution)/shard_map/ppermute | solution.py:354
  24.7 0.6 copy-done.35
  25.3 0.6 copy-done.36
  25.9 15.3 %shard_map.121 = (f32[528,128]{1,0:T(8,128)}, f32[528,128]{1,0:T(8,128)}, f32[528,128]{1,0:T(8,128)}, f32[528,128]{1,0:T(8,128)}, f32[64,512]{1,0:T(8,128)}, /*i...) custom-call(bf16[112,512]{1,0:T(8,128)(2,1)} %get-tuple-element.64.own, bf16[112,512]{1,0:T(8,128)(2,1)} %copy-done.31, ...), custom_call_target="tpu_custom_call" | custom-call | flops 12000000000 | bytes 3637248 | tf_op jit(solution)/shard_map/pallas_call | solution.py:31
  41.3 0.5 collective-permute-start.13
  41.8 1.2 %collective-permute-done.14 = f32[528,128]{1,0:T(8,128)S(1)} collective-permute-done((f32[528,128]{1,0:T(8,128)}, f32[528,128]{1,0:T(8,128)S(1)}, u32[]{:S(2)}, u32[]{:S(2)}) %collective-permute-start.14) | collective-permute-done | bytes 270368 | tf_op jit(solution)/shard_map/ppermute | solution.py:351
  43.0 1.0 add.28
  44.0 1.5 %collective-permute-start.15 = (f32[528,128]{1,0:T(8,128)S(1)}, f32[528,128]{1,0:T(8,128)S(1)}, u32[]{:S(2)}, u32[]{:S(2)}) collective-permute-start(f32[528,128]{1,0:T(8,128)S(1)} %add.28), channel_id=1, source_target_pairs={{0,16},{4,20},{8,24},{12,28},{16,0},{20,4},{24,8},{28,12},{1,17},{... | collective-permute-start | bytes 811016 | tf_op jit(solution)/shard_map/ppermute | solution.py:351
  45.5 0.7 collective-permute-start.10
  46.2 3.1 %collective-permute-start.11 = (f32[64,512]{1,0:T(8,128)}, f32[64,512]{1,0:T(8,128)S(1)}, u32[]{:S(2)}, u32[]{:S(2)}) collective-permute-start(f32[64,512]{1,0:T(8,128)} %get-tuple-element.71), channel_id=1, source_target_pairs={{0,2},{1,3},{2,0},{3,1},{4,6},{5,7},{6,4},{7,5},{8,10},{9,11},{10,... | collective-permute-start | bytes 393224 | tf_op jit(solution)/shard_map/ppermute | solution.py:357
  49.3 0.6 collective-permute-start.12
  49.9 2.9 %shard_map.122 = (f32[512,128]{1,0:T(8,128)}, bf16[768,256]{1,0:T(8,128)(2,1)}, bf16[768,512]{1,0:T(8,128)(2,1)}) custom-call(bf16[64,768]{1,0:T(8,128)(2,1)} %refs_0_, bf16[64,768]{1,0:T(8,128)(2,1)} %copy-done.25, bf16[64,768]{1,0:T(8,128)(2,1)} %copy-done.24, bf16[64,768]{1,0:T(8,128)(2,1)} %copy-done.26, bf16[128,768]{1,0:T(8,128)(2,1)} %refs_4_, ...), custom_call_target="tpu_custom_call" | custom-call | flops 100663296 | bytes 3407872 | tf_op jit(solution)/shard_map/pallas_call | solution.py:31
  53.0 6.5 %collective-permute-done.11.c = f32[64,512]{1,0:T(8,128)S(1)} collective-permute-done((f32[64,512]{1,0:T(8,128)}, f32[64,512]{1,0:T(8,128)S(1)}, u32[]{:S(2)}, u32[]{:S(2)}) %collective-permute-start.11) | collective-permute-done | bytes 131104 | tf_op jit(solution)/shard_map/ppermute | solution.py:357
  59.5 0.6 copy-done.8
  60.2 1.9 %shard_map.123 = (f32[64,512]{1,0:T(8,128)}, bf16[64,128]{1,0:T(8,128)(2,1)}, bf16[64,128]{1,0:T(8,128)(2,1)}, bf16[64,128]{1,0:T(8,128)(2,1)}, bf16[64,128]{1,0:T(8,128)(2,1)}) custom-call(f32[64,512]{1,0:T(8,128)} %get-tuple-element.83.a, f32[64,512]{1,0:T(8,128)} %copy-done.7, f32[64,512]{1,0:T(8,128)} %copy-done.8, f32[64,512]{1,0:T(8,128)} %copy-done.9, ...), custom_call_target="tpu_custom_call" | custom-call | bytes 851968 | tf_op jit(solution)/shard_map/pallas_call | solution.py:31
  62.2 0.7 collective-permute-start.20
  62.9 1.2 %collective-permute-start.21 = (bf16[64,128]{1,0:T(8,128)(2,1)}, bf16[64,128]{1,0:T(8,128)(2,1)S(1)}, u32[]{:S(2)}, u32[]{:S(2)}) collective-permute-start(bf16[64,128]{1,0:T(8,128)(2,1)} %get-tuple-element.110), channel_id=1, source_target_pairs={{0,20},{4,16},{8,28},{12,24},{16,4},{20,0},{24,12},{28,8},{1,21},{... | collective-permute-start | bytes 49160 | tf_op jit(solution)/shard_map/ppermute | solution.py:351
  64.0 2.9 %shard_map.124 = (f32[400,128]{1,0:T(8,128)}, f32[400,128]{1,0:T(8,128)}, f32[128,128]{1,0:T(8,128)}, f32[128,128]{1,0:T(8,128)}, f32[128,128]{1,0:T(8,128)}, /*index=5*/f32[128,128]{1,0:T(8,128)}) custom-call(f32[528,128]{1,0:T(8,128)} %get-tuple-element.89.keep, f32[528,128]{1,0:T(8,128)} %copy-done.2, f32[528,128]{1,0:T(8,128)} %copy-done.3, ...), custom_call_target="tpu_custom_call" | custom-call | flops 100663296 | bytes 2531328 | tf_op jit(solution)/shard_map/pallas_call | solution.py:31
  67.0 0.6 copy-done.32
  67.6 2.2 %shard_map.125 = (f32[208,128]{1,0:T(8,128)}, f32[192,128]{1,0:T(8,128)}, f32[208,128]{1,0:T(8,128)}, f32[192,128]{1,0:T(8,128)}) custom-call(f32[400,128]{1,0:T(8,128)} %get-tuple-element.104.keep_in, f32[400,128]{1,0:T(8,128)} %get-tuple-element.105.send_in, bf16[768,256]{1,0:T(8,128)(2,1)} %get-tuple-element.106.turned, ...), custom_call_target="tpu_custom_call" | custom-call | flops 50331648 | bytes 1277952 | tf_op jit(solution)/shard_map/pallas_call | solution.py:31
  69.8 1.5 %collective-permute-start.28 = (f32[192,128]{1,0:T(8,128)}, f32[192,128]{1,0:T(8,128)S(1)}, u32[]{:S(2)}, u32[]{:S(2)}) collective-permute-start(f32[192,128]{1,0:T(8,128)} %get-tuple-element.121), channel_id=1, source_target_pairs={{0,8},{4,12},{8,0},{12,4},{16,24},{20,28},{24,16},{28,20},{1,9},{5... | collective-permute-start | bytes 294920 | tf_op jit(solution)/shard_map/ppermute | solution.py:351
  71.3 0.5 collective-permute-start.22
  71.9 3.9 %collective-permute-done.28 = f32[192,128]{1,0:T(8,128)S(1)} collective-permute-done((f32[192,128]{1,0:T(8,128)}, f32[192,128]{1,0:T(8,128)S(1)}, u32[]{:S(2)}, u32[]{:S(2)}) %collective-permute-start.28) | collective-permute-done | bytes 98336 | tf_op jit(solution)/shard_map/ppermute | solution.py:351
  75.7 0.9 add.32
  76.6 2.6 %collective-permute-start.29 = (f32[192,128]{1,0:T(8,128)S(1)}, f32[192,128]{1,0:T(8,128)S(1)}, u32[]{:S(2)}, u32[]{:S(2)}) collective-permute-start(f32[192,128]{1,0:T(8,128)S(1)} %add.32), channel_id=1, source_target_pairs={{0,3},{1,2},{2,1},{3,0},{4,7},{5,6},{6,5},{7,4},{8,11},{9,10},{10,... | collective-permute-start | bytes 294920 | tf_op jit(solution)/shard_map/ppermute | solution.py:357
  79.2 0.6 collective-permute-start.17
  79.9 1.2 %collective-permute-start.18 = (f32[128,128]{1,0:T(8,128)}, f32[128,128]{1,0:T(8,128)S(1)}, u32[]{:S(2)}, u32[]{:S(2)}) collective-permute-start(f32[128,128]{1,0:T(8,128)} %get-tuple-element.103), channel_id=1, source_target_pairs={{0,20},{4,16},{8,28},{12,24},{16,4},{20,0},{24,12},{28,8},{1,21},{... | collective-permute-start | bytes 196616 | tf_op jit(solution)/shard_map/ppermute | solution.py:351
  81.1 3.3 %collective-permute-done.17.refs_2_ = f32[128,128]{1,0:T(8,128)S(1)} collective-permute-done((f32[128,128]{1,0:T(8,128)}, f32[128,128]{1,0:T(8,128)S(1)}, u32[]{:S(2)}, u32[]{:S(2)}) %collective-permute-start.17) | collective-permute-done | bytes 65568 | tf_op jit(solution)/shard_map/ppermute | solution.py:351
  84.4 0.5 collective-permute-done.18.refs_3_
  84.9 0.9 add.29
  85.8 1.2 %collective-permute-start.23 = (f32[208,128]{1,0:T(8,128)S(1)}, f32[208,128]{1,0:T(8,128)S(1)}, u32[]{:S(2)}, u32[]{:S(2)}) collective-permute-start(f32[208,128]{1,0:T(8,128)S(1)} %add.29), channel_id=1, source_target_pairs={{0,1},{1,0},{2,3},{3,2},{4,5},{5,4},{6,7},{7,6},{8,9},{9,8},{10,11... | collective-permute-start | bytes 319496 | tf_op jit(solution)/shard_map/ppermute | solution.py:357
  87.1 0.9 collective-permute-start.30
  88.0 1.7 %shard_map.126 = f32[128,512]{1,0:T(8,128)} custom-call(f32[128,128]{1,0:T(8,128)} %get-tuple-element.112.refs_0_, f32[128,128]{1,0:T(8,128)} %copy-done.27, f32[128,128]{1,0:T(8,128)} %copy-done.28, f32[128,128]{1,0:T(8,128)} %copy-done.29), custom_call_target="tpu_custom_call" | custom-call | bytes 524288 | tf_op jit(solution)/shard_map/pallas_call | solution.py:31
  89.7 2.0 %collective-permute-done.23 = f32[208,128]{1,0:T(8,128)S(1)} collective-permute-done((f32[208,128]{1,0:T(8,128)S(1)}, f32[208,128]{1,0:T(8,128)S(1)}, u32[]{:S(2)}, u32[]{:S(2)}) %collective-permute-start.23) | collective-permute-done | bytes 106528 | tf_op jit(solution)/shard_map/ppermute | solution.py:357
  91.7 1.4 %collective-permute-start.24 = (f32[208,128]{1,0:T(8,128)S(1)}, f32[208,128]{1,0:T(8,128)S(1)}, u32[]{:S(2)}, u32[]{:S(2)}) collective-permute-start(f32[208,128]{1,0:T(8,128)S(1)} %add.30), channel_id=1, source_target_pairs={{0,3},{1,2},{2,1},{3,0},{4,7},{5,6},{6,5},{7,4},{8,11},{9,10},{10,... | collective-permute-start | bytes 319496 | tf_op jit(solution)/shard_map/ppermute | solution.py:357
  93.2 1.8 %collective-permute-start.40 = (f32[192,128]{1,0:T(8,128)S(1)}, f32[192,128]{1,0:T(8,128)S(1)}, u32[]{:S(2)}, u32[]{:S(2)}) collective-permute-start(f32[192,128]{1,0:T(8,128)S(1)} %add.34.refs_4_), channel_id=1, source_target_pairs={{0,24},{4,28},{8,16},{12,20},{16,8},{20,12},{24,0},{28,4},{1,25},{... | collective-permute-start | bytes 294920 | tf_op jit(solution)/shard_map/ppermute | solution.py:351
  95.0 0.5 collective-permute-start.38
  95.5 1.3 %collective-permute-start.32 = (f32[192,128]{1,0:T(8,128)S(1)}, f32[192,128]{1,0:T(8,128)S(1)}, u32[]{:S(2)}, u32[]{:S(2)}) collective-permute-start(f32[192,128]{1,0:T(8,128)S(1)} %add.34.refs_4_), channel_id=1, source_target_pairs={{0,16},{4,20},{8,24},{12,28},{16,0},{20,4},{24,8},{28,12},{1,17},{... | collective-permute-start | bytes 294920 | tf_op jit(solution)/shard_map/ppermute | solution.py:351
  96.7 1.6 %collective-permute-done.24 = f32[208,128]{1,0:T(8,128)S(1)} collective-permute-done((f32[208,128]{1,0:T(8,128)S(1)}, f32[208,128]{1,0:T(8,128)S(1)}, u32[]{:S(2)}, u32[]{:S(2)}) %collective-permute-start.24) | collective-permute-done | bytes 106528 | tf_op jit(solution)/shard_map/ppermute | solution.py:357
  98.4 1.8 %collective-permute-start.36 = (f32[208,128]{1,0:T(8,128)S(1)}, f32[208,128]{1,0:T(8,128)S(1)}, u32[]{:S(2)}, u32[]{:S(2)}) collective-permute-start(f32[208,128]{1,0:T(8,128)S(1)} %add.31.refs_0_), channel_id=1, source_target_pairs={{0,24},{4,28},{8,16},{12,20},{16,8},{20,12},{24,0},{28,4},{1,25},{... | collective-permute-start | bytes 319496 | tf_op jit(solution)/shard_map/ppermute | solution.py:351
  100.2 0.6 collective-permute-start.34
  100.8 1.1 %collective-permute-start.26 = (f32[208,128]{1,0:T(8,128)S(1)}, f32[208,128]{1,0:T(8,128)S(1)}, u32[]{:S(2)}, u32[]{:S(2)}) collective-permute-start(f32[208,128]{1,0:T(8,128)S(1)} %add.31.refs_0_), channel_id=1, source_target_pairs={{0,16},{4,20},{8,24},{12,28},{16,0},{20,4},{24,8},{28,12},{1,17},{... | collective-permute-start | bytes 319496 | tf_op jit(solution)/shard_map/ppermute | solution.py:351
  102.0 0.5 collective-permute-start.41
  102.5 1.8 %collective-permute-done.36.refs_10_ = f32[208,128]{1,0:T(8,128)S(1)} collective-permute-done((f32[208,128]{1,0:T(8,128)S(1)}, f32[208,128]{1,0:T(8,128)S(1)}, u32[]{:S(2)}, u32[]{:S(2)}) %collective-permute-start.36) | collective-permute-done | bytes 106528 | tf_op jit(solution)/shard_map/ppermute | solution.py:351
  104.3 0.6 collective-permute-done.34.refs_8_
  104.9 0.6 collective-permute-done.26.refs_2_
  105.5 0.5 collective-permute-start.39
  106.1 0.9 collective-permute-done.39.refs_13_
  107.0 0.4 collective-permute-done.33.refs_7_
  107.5 0.1 copy-done.22
  107.6 0.3 copy-done.23
  108.1 0.6 copy-done.16
  108.7 2.8 %shard_map.127 = (f32[768,512]{1,0:T(8,128)}, f32[3,512]{1,0:T(4,128)}) custom-call(f32[208,128]{1,0:T(8,128)} %copy-done, f32[208,128]{1,0:T(8,128)} %copy-done.13, f32[208,128]{1,0:T(8,128)} %copy-done.12, f32[208,128]{1,0:T(8,128)} %copy-done.16, f32[192,128]{1,0:T(8,128)} %copy-done.1, f32[192,128]{1,0:T(8,128)} %copy-done.20, f32[192,128]{1,0:T(8,128)} %copy-done.19, ...), custom_call_target="tpu_custom_call" | custom-call | bytes 3217408 | tf_op jit(solution)/shard_map/pallas_call | solution.py:31
  (112 shorter events, 0.9 us)
Async XLA Ops:
  0.6 14.2 %collective-permute-start.8 = (bf16[64,768]{1,0:T(8,128)(2,1)}, bf16[64,768]{1,0:T(8,128)(2,1)S(1)}, u32[]{:S(2)}, u32[]{:S(2)}) collective-permute-start(bf16[64,768]{1,0:T(8,128)(2,1)} %refs_0_), channel_id=1, source_target_pairs={{0,16},{4,20},{8,24},{12,28},{16,0},{20,4},{24,8},{28,12},{1,17},{... | collective-permute-start | bytes 294920 | tf_op jit(solution)/shard_map/ppermute | solution.py:351
  3.7 7.2 %collective-permute-start.5 = (bf16[128,768]{1,0:T(8,128)(2,1)}, bf16[128,768]{1,0:T(8,128)(2,1)S(1)}, u32[]{:S(2)}, u32[]{:S(2)}) collective-permute-start(bf16[128,768]{1,0:T(8,128)(2,1)} %refs_4_), channel_id=1, source_target_pairs={{0,16},{4,20},{8,24},{12,28},{16,0},{20,4},{24,8},{28,12},{1,17},{... | collective-permute-start | bytes 589832 | tf_op jit(solution)/shard_map/ppermute | solution.py:351
  7.2 7.8 %collective-permute-start.1 = (bf16[112,512]{1,0:T(8,128)(2,1)}, bf16[112,512]{1,0:T(8,128)(2,1)S(1)}, u32[]{:S(2)}, u32[]{:S(2)}) collective-permute-start(bf16[112,512]{1,0:T(8,128)(2,1)} %get-tuple-element.64.own), channel_id=1, source_target_pairs={{0,1},{1,2},{2,3},{3,0},{4,5},{5,6},{6,7},{7,4},{8,9},{9,10},{10,1... | collective-permute-start | bytes 344072 | tf_op jit(solution)/shard_map/ppermute | solution.py:354
  9.2 13.2 %collective-permute-start.4 = (bf16[128,768]{1,0:T(8,128)(2,1)}, bf16[128,768]{1,0:T(8,128)(2,1)S(1)}, u32[]{:S(2)}, u32[]{:S(2)}) collective-permute-start(bf16[128,768]{1,0:T(8,128)(2,1)} %refs_4_), channel_id=1, source_target_pairs={{0,4},{4,0},{8,12},{12,8},{16,20},{20,16},{24,28},{28,24},{1,5},{5... | collective-permute-start | bytes 589832 | tf_op jit(solution)/shard_map/ppermute | solution.py:351
  10.9 13.8 %copy-start.4 = (bf16[128,768]{1,0:T(8,128)(2,1)}, bf16[128,768]{1,0:T(8,128)(2,1)S(1)}, u32[]{:S(2)}) copy-start(bf16[128,768]{1,0:T(8,128)(2,1)S(1)} %collective-permute-done.5.f_high.refs_6_) | copy-start | bytes 589828
  10.9 11.6 %collective-permute-start.6 = (bf16[128,768]{1,0:T(8,128)(2,1)S(1)}, bf16[128,768]{1,0:T(8,128)(2,1)S(1)}, u32[]{:S(2)}, u32[]{:S(2)}) collective-permute-start(bf16[128,768]{1,0:T(8,128)(2,1)S(1)} %collective-permute-done.5.f_high.refs_6_), channel_id=1, source_target_pairs={{0,4},{4,0},{8,12},{12,8},{16,20},{20,16},{24,28},{28,24},{1,5},{5... | collective-permute-start | bytes 589832 | tf_op jit(solution)/shard_map/ppermute | solution.py:351
  10.9 7.3 %collective-permute-start = (bf16[112,512]{1,0:T(8,128)(2,1)}, bf16[112,512]{1,0:T(8,128)(2,1)S(1)}, u32[]{:S(2)}, u32[]{:S(2)}) collective-permute-start(bf16[112,512]{1,0:T(8,128)(2,1)} %get-tuple-element.64.own), channel_id=1, source_target_pairs={{0,3},{1,0},{2,1},{3,2},{4,7},{5,4},{6,5},{7,6},{8,11},{9,8},{10,9... | collective-permute-start | bytes 344072 | tf_op jit(solution)/shard_map/ppermute | solution.py:354
  14.8 26.4 %copy-start.24 = (bf16[64,768]{1,0:T(8,128)(2,1)}, bf16[64,768]{1,0:T(8,128)(2,1)S(1)}, u32[]{:S(2)}) copy-start(bf16[64,768]{1,0:T(8,128)(2,1)S(1)} %collective-permute-done.8.refs_2_) | copy-start | bytes 294916
  14.8 3.7 %collective-permute-start.7 = (bf16[64,768]{1,0:T(8,128)(2,1)}, bf16[64,768]{1,0:T(8,128)(2,1)S(1)}, u32[]{:S(2)}, u32[]{:S(2)}) collective-permute-start(bf16[64,768]{1,0:T(8,128)(2,1)} %refs_0_), channel_id=1, source_target_pairs={{0,4},{4,0},{8,12},{12,8},{16,20},{20,16},{24,28},{28,24},{1,5},{5... | collective-permute-start | bytes 294920 | tf_op jit(solution)/shard_map/ppermute | solution.py:351
  15.1 9.6 %copy-start.30 = (bf16[112,512]{1,0:T(8,128)(2,1)}, bf16[112,512]{1,0:T(8,128)(2,1)S(1)}, u32[]{:S(2)}) copy-start(bf16[112,512]{1,0:T(8,128)(2,1)S(1)} %collective-permute-done.1.minus) | copy-start | bytes 344068
  15.1 7.4 %collective-permute-start.9 = (bf16[64,768]{1,0:T(8,128)(2,1)S(1)}, bf16[64,768]{1,0:T(8,128)(2,1)S(1)}, u32[]{:S(2)}, u32[]{:S(2)}) collective-permute-start(bf16[64,768]{1,0:T(8,128)(2,1)S(1)} %collective-permute-done.8.refs_2_), channel_id=1, source_target_pairs={{0,4},{4,0},{8,12},{12,8},{16,20},{20,16},{24,28},{28,24},{1,5},{5... | collective-permute-start | bytes 294920 | tf_op jit(solution)/shard_map/ppermute | solution.py:351
  18.2 6.5 %copy-start.31 = (bf16[112,512]{1,0:T(8,128)(2,1)}, bf16[112,512]{1,0:T(8,128)(2,1)S(1)}, u32[]{:S(2)}) copy-start(bf16[112,512]{1,0:T(8,128)(2,1)S(1)} %collective-permute-done.plus) | copy-start | bytes 344068
  18.2 6.4 %collective-permute-start.3 = (bf16[56,512]{1,0:T(8,128)(2,1)S(1)}, bf16[56,512]{1,0:T(8,128)(2,1)S(1)}, u32[]{:S(2)}, u32[]{:S(2)}) collective-permute-start(bf16[56,512]{1,0:T(8,128)(2,1)S(1)} %slice.17), channel_id=1, source_target_pairs={{0,1},{1,2},{2,3},{3,0},{4,5},{5,6},{6,7},{7,4},{8,9},{9,10},{10,1... | collective-permute-start | bytes 172040 | tf_op jit(solution)/shard_map/ppermute | solution.py:354
  18.6 22.6 %copy-start.25 = (bf16[64,768]{1,0:T(8,128)(2,1)}, bf16[64,768]{1,0:T(8,128)(2,1)S(1)}, u32[]{:S(2)}) copy-start(bf16[64,768]{1,0:T(8,128)(2,1)S(1)} %collective-permute-done.7.refs_1_) | copy-start | bytes 294916
  18.6 6.1 %collective-permute-start.2 = (bf16[56,512]{1,0:T(8,128)(2,1)S(1)}, bf16[56,512]{1,0:T(8,128)(2,1)S(1)}, u32[]{:S(2)}, u32[]{:S(2)}) collective-permute-start(bf16[56,512]{1,0:T(8,128)(2,1)S(1)} %slice.16), channel_id=1, source_target_pairs={{0,3},{1,0},{2,1},{3,2},{4,7},{5,4},{6,5},{7,6},{8,11},{9,8},{10,9... | collective-permute-start | bytes 172040 | tf_op jit(solution)/shard_map/ppermute | solution.py:354
  22.5 18.7 %copy-start.26 = (bf16[64,768]{1,0:T(8,128)(2,1)}, bf16[64,768]{1,0:T(8,128)(2,1)S(1)}, u32[]{:S(2)}) copy-start(bf16[64,768]{1,0:T(8,128)(2,1)S(1)} %collective-permute-done.9.refs_3_) | copy-start | bytes 294916
  22.5 2.2 %copy-start.5 = (bf16[128,768]{1,0:T(8,128)(2,1)}, bf16[128,768]{1,0:T(8,128)(2,1)S(1)}, u32[]{:S(2)}) copy-start(bf16[128,768]{1,0:T(8,128)(2,1)S(1)} %collective-permute-done.4.f_low.refs_5_) | copy-start | bytes 589828
  22.5 2.2 %copy-start.6 = (bf16[128,768]{1,0:T(8,128)(2,1)}, bf16[128,768]{1,0:T(8,128)(2,1)S(1)}, u32[]{:S(2)}) copy-start(bf16[128,768]{1,0:T(8,128)(2,1)S(1)} %collective-permute-done.6.f_far.refs_7_) | copy-start | bytes 589828
  41.2 1.8 %collective-permute-start.14 = (f32[528,128]{1,0:T(8,128)}, f32[528,128]{1,0:T(8,128)S(1)}, u32[]{:S(2)}, u32[]{:S(2)}) collective-permute-start(f32[528,128]{1,0:T(8,128)} %get-tuple-element.96), channel_id=1, source_target_pairs={{0,4},{4,0},{8,12},{12,8},{16,20},{20,16},{24,28},{28,24},{1,5},{5... | collective-permute-start | bytes 811016 | tf_op jit(solution)/shard_map/ppermute | solution.py:351
  41.3 8.6 %collective-permute-start.13 = (f32[528,128]{1,0:T(8,128)}, f32[528,128]{1,0:T(8,128)S(1)}, u32[]{:S(2)}, u32[]{:S(2)}) collective-permute-start(f32[528,128]{1,0:T(8,128)} %get-tuple-element.77), channel_id=1, source_target_pairs={{0,4},{4,0},{8,12},{12,8},{16,20},{20,16},{24,28},{28,24},{1,5},{5... | collective-permute-start | bytes 811016 | tf_op jit(solution)/shard_map/ppermute | solution.py:351
  44.0 18.1 %collective-permute-start.15 = (f32[528,128]{1,0:T(8,128)S(1)}, f32[528,128]{1,0:T(8,128)S(1)}, u32[]{:S(2)}, u32[]{:S(2)}) collective-permute-start(f32[528,128]{1,0:T(8,128)S(1)} %add.28), channel_id=1, source_target_pairs={{0,16},{4,20},{8,24},{12,28},{16,0},{20,4},{24,8},{28,12},{1,17},{... | collective-permute-start | bytes 811016 | tf_op jit(solution)/shard_map/ppermute | solution.py:351
  45.5 7.4 %collective-permute-start.10 = (f32[64,512]{1,0:T(8,128)}, f32[64,512]{1,0:T(8,128)S(1)}, u32[]{:S(2)}, u32[]{:S(2)}) collective-permute-start(f32[64,512]{1,0:T(8,128)} %get-tuple-element.70), channel_id=1, source_target_pairs={{0,1},{1,0},{2,3},{3,2},{4,5},{5,4},{6,7},{7,6},{8,9},{9,8},{10,11... | collective-permute-start | bytes 393224 | tf_op jit(solution)/shard_map/ppermute | solution.py:357
  46.2 13.3 %collective-permute-start.11 = (f32[64,512]{1,0:T(8,128)}, f32[64,512]{1,0:T(8,128)S(1)}, u32[]{:S(2)}, u32[]{:S(2)}) collective-permute-start(f32[64,512]{1,0:T(8,128)} %get-tuple-element.71), channel_id=1, source_target_pairs={{0,2},{1,3},{2,0},{3,1},{4,6},{5,7},{6,4},{7,5},{8,10},{9,11},{10,... | collective-permute-start | bytes 393224 | tf_op jit(solution)/shard_map/ppermute | solution.py:357
  49.3 10.2 %collective-permute-start.12 = (f32[64,512]{1,0:T(8,128)}, f32[64,512]{1,0:T(8,128)S(1)}, u32[]{:S(2)}, u32[]{:S(2)}) collective-permute-start(f32[64,512]{1,0:T(8,128)} %get-tuple-element.72), channel_id=1, source_target_pairs={{0,3},{1,2},{2,1},{3,0},{4,7},{5,6},{6,5},{7,4},{8,11},{9,10},{10,... | collective-permute-start | bytes 393224 | tf_op jit(solution)/shard_map/ppermute | solution.py:357
  49.9 14.1 %copy-start.2 = (f32[528,128]{1,0:T(8,128)}, f32[528,128]{1,0:T(8,128)S(1)}, u32[]{:S(2)}) copy-start(f32[528,128]{1,0:T(8,128)S(1)} %collective-permute-done.13.recv) | copy-start | bytes 811012
  53.0 6.5 %copy-start.7 = (f32[64,512]{1,0:T(8,128)}, f32[64,512]{1,0:T(8,128)S(1)}, u32[]{:S(2)}) copy-start(f32[64,512]{1,0:T(8,128)S(1)} %collective-permute-done.10.b) | copy-start | bytes 393220
  62.1 4.9 %collective-permute-start.19 = (bf16[64,128]{1,0:T(8,128)(2,1)}, bf16[64,128]{1,0:T(8,128)(2,1)S(1)}, u32[]{:S(2)}, u32[]{:S(2)}) collective-permute-start(bf16[64,128]{1,0:T(8,128)(2,1)} %get-tuple-element.108), channel_id=1, source_target_pairs={{0,4},{4,0},{8,12},{12,8},{16,20},{20,16},{24,28},{28,24},{1,5},{5... | collective-permute-start | bytes 49160 | tf_op jit(solution)/shard_map/ppermute | solution.py:351
  62.2 4.8 %collective-permute-start.20 = (bf16[64,128]{1,0:T(8,128)(2,1)}, bf16[64,128]{1,0:T(8,128)(2,1)S(1)}, u32[]{:S(2)}, u32[]{:S(2)}) collective-permute-start(bf16[64,128]{1,0:T(8,128)(2,1)} %get-tuple-element.109), channel_id=1, source_target_pairs={{0,16},{4,20},{8,24},{12,28},{16,0},{20,4},{24,8},{28,12},{1,17},{... | collective-permute-start | bytes 49160 | tf_op jit(solution)/shard_map/ppermute | solution.py:351
  62.9 4.1 %collective-permute-start.21 = (bf16[64,128]{1,0:T(8,128)(2,1)}, bf16[64,128]{1,0:T(8,128)(2,1)S(1)}, u32[]{:S(2)}, u32[]{:S(2)}) collective-permute-start(bf16[64,128]{1,0:T(8,128)(2,1)} %get-tuple-element.110), channel_id=1, source_target_pairs={{0,20},{4,16},{8,28},{12,24},{16,4},{20,0},{24,12},{28,8},{1,21},{... | collective-permute-start | bytes 49160 | tf_op jit(solution)/shard_map/ppermute | solution.py:351
  69.8 5.9 %collective-permute-start.28 = (f32[192,128]{1,0:T(8,128)}, f32[192,128]{1,0:T(8,128)S(1)}, u32[]{:S(2)}, u32[]{:S(2)}) collective-permute-start(f32[192,128]{1,0:T(8,128)} %get-tuple-element.121), channel_id=1, source_target_pairs={{0,8},{4,12},{8,0},{12,4},{16,24},{20,28},{24,16},{28,20},{1,9},{5... | collective-permute-start | bytes 294920 | tf_op jit(solution)/shard_map/ppermute | solution.py:351
  71.3 13.6 %collective-permute-start.22 = (f32[208,128]{1,0:T(8,128)}, f32[208,128]{1,0:T(8,128)S(1)}, u32[]{:S(2)}, u32[]{:S(2)}) collective-permute-start(f32[208,128]{1,0:T(8,128)} %get-tuple-element.111), channel_id=1, source_target_pairs={{0,8},{4,12},{8,0},{12,4},{16,24},{20,28},{24,16},{28,20},{1,9},{5... | collective-permute-start | bytes 319496 | tf_op jit(solution)/shard_map/ppermute | solution.py:351
  76.6 10.4 %collective-permute-start.29 = (f32[192,128]{1,0:T(8,128)S(1)}, f32[192,128]{1,0:T(8,128)S(1)}, u32[]{:S(2)}, u32[]{:S(2)}) collective-permute-start(f32[192,128]{1,0:T(8,128)S(1)} %add.32), channel_id=1, source_target_pairs={{0,3},{1,2},{2,1},{3,0},{4,7},{5,6},{6,5},{7,4},{8,11},{9,10},{10,... | collective-permute-start | bytes 294920 | tf_op jit(solution)/shard_map/ppermute | solution.py:357
  79.2 1.9 %collective-permute-start.16 = (f32[128,128]{1,0:T(8,128)}, f32[128,128]{1,0:T(8,128)S(1)}, u32[]{:S(2)}, u32[]{:S(2)}) collective-permute-start(f32[128,128]{1,0:T(8,128)} %get-tuple-element.101), channel_id=1, source_target_pairs={{0,4},{4,0},{8,12},{12,8},{16,20},{20,16},{24,28},{28,24},{1,5},{5... | collective-permute-start | bytes 196616 | tf_op jit(solution)/shard_map/ppermute | solution.py:351
  79.2 5.2 %collective-permute-start.17 = (f32[128,128]{1,0:T(8,128)}, f32[128,128]{1,0:T(8,128)S(1)}, u32[]{:S(2)}, u32[]{:S(2)}) collective-permute-start(f32[128,128]{1,0:T(8,128)} %get-tuple-element.102), channel_id=1, source_target_pairs={{0,16},{4,20},{8,24},{12,28},{16,0},{20,4},{24,8},{28,12},{1,17},{... | collective-permute-start | bytes 196616 | tf_op jit(solution)/shard_map/ppermute | solution.py:351
  79.9 5.0 %collective-permute-start.18 = (f32[128,128]{1,0:T(8,128)}, f32[128,128]{1,0:T(8,128)S(1)}, u32[]{:S(2)}, u32[]{:S(2)}) collective-permute-start(f32[128,128]{1,0:T(8,128)} %get-tuple-element.103), channel_id=1, source_target_pairs={{0,20},{4,16},{8,28},{12,24},{16,4},{20,0},{24,12},{28,8},{1,21},{... | collective-permute-start | bytes 196616 | tf_op jit(solution)/shard_map/ppermute | solution.py:351
  81.1 6.9 %copy-start.27 = (f32[128,128]{1,0:T(8,128)}, f32[128,128]{1,0:T(8,128)S(1)}, u32[]{:S(2)}) copy-start(f32[128,128]{1,0:T(8,128)S(1)} %collective-permute-done.16.refs_1_) | copy-start | bytes 196612
  84.4 3.6 %copy-start.28 = (f32[128,128]{1,0:T(8,128)}, f32[128,128]{1,0:T(8,128)S(1)}, u32[]{:S(2)}) copy-start(f32[128,128]{1,0:T(8,128)S(1)} %collective-permute-done.17.refs_2_) | copy-start | bytes 196612
  84.9 3.1 %copy-start.29 = (f32[128,128]{1,0:T(8,128)}, f32[128,128]{1,0:T(8,128)S(1)}, u32[]{:S(2)}) copy-start(f32[128,128]{1,0:T(8,128)S(1)} %collective-permute-done.18.refs_3_) | copy-start | bytes 196612
  85.8 5.9 %collective-permute-start.23 = (f32[208,128]{1,0:T(8,128)S(1)}, f32[208,128]{1,0:T(8,128)S(1)}, u32[]{:S(2)}, u32[]{:S(2)}) collective-permute-start(f32[208,128]{1,0:T(8,128)S(1)} %add.29), channel_id=1, source_target_pairs={{0,1},{1,0},{2,3},{3,2},{4,5},{5,4},{6,7},{7,6},{8,9},{9,8},{10,11... | collective-permute-start | bytes 319496 | tf_op jit(solution)/shard_map/ppermute | solution.py:357
  87.1 6.1 %collective-permute-start.30 = (f32[192,128]{1,0:T(8,128)S(1)}, f32[192,128]{1,0:T(8,128)S(1)}, u32[]{:S(2)}, u32[]{:S(2)}) collective-permute-start(f32[192,128]{1,0:T(8,128)S(1)} %add.33), channel_id=1, source_target_pairs={{0,1},{1,0},{2,3},{3,2},{4,5},{5,4},{6,7},{7,6},{8,9},{9,8},{10,11... | collective-permute-start | bytes 294920 | tf_op jit(solution)/shard_map/ppermute | solution.py:357
  91.7 6.6 %collective-permute-start.24 = (f32[208,128]{1,0:T(8,128)S(1)}, f32[208,128]{1,0:T(8,128)S(1)}, u32[]{:S(2)}, u32[]{:S(2)}) collective-permute-start(f32[208,128]{1,0:T(8,128)S(1)} %add.30), channel_id=1, source_target_pairs={{0,3},{1,2},{2,1},{3,0},{4,7},{5,6},{6,5},{7,4},{8,11},{9,10},{10,... | collective-permute-start | bytes 319496 | tf_op jit(solution)/shard_map/ppermute | solution.py:357
  93.2 14.2 %copy-start.1 = (f32[192,128]{1,0:T(8,128)}, f32[192,128]{1,0:T(8,128)S(1)}, u32[]{:S(2)}) copy-start(f32[192,128]{1,0:T(8,128)S(1)} %add.34.refs_4_) | copy-start | bytes 294916
  93.2 7.0 %collective-permute-start.40 = (f32[192,128]{1,0:T(8,128)S(1)}, f32[192,128]{1,0:T(8,128)S(1)}, u32[]{:S(2)}, u32[]{:S(2)}) collective-permute-start(f32[192,128]{1,0:T(8,128)S(1)} %add.34.refs_4_), channel_id=1, source_target_pairs={{0,24},{4,28},{8,16},{12,20},{16,8},{20,12},{24,0},{28,4},{1,25},{... | collective-permute-start | bytes 294920 | tf_op jit(solution)/shard_map/ppermute | solution.py:351
  95.0 5.9 %collective-permute-start.38 = (f32[192,128]{1,0:T(8,128)S(1)}, f32[192,128]{1,0:T(8,128)S(1)}, u32[]{:S(2)}, u32[]{:S(2)}) collective-permute-start(f32[192,128]{1,0:T(8,128)S(1)} %add.34.refs_4_), channel_id=1, source_target_pairs={{0,8},{4,12},{8,0},{12,4},{16,24},{20,28},{24,16},{28,20},{1,9},{5... | collective-permute-start | bytes 294920 | tf_op jit(solution)/shard_map/ppermute | solution.py:351
  95.5 6.5 %collective-permute-start.32 = (f32[192,128]{1,0:T(8,128)S(1)}, f32[192,128]{1,0:T(8,128)S(1)}, u32[]{:S(2)}, u32[]{:S(2)}) collective-permute-start(f32[192,128]{1,0:T(8,128)S(1)} %add.34.refs_4_), channel_id=1, source_target_pairs={{0,16},{4,20},{8,24},{12,28},{16,0},{20,4},{24,8},{28,12},{1,17},{... | collective-permute-start | bytes 294920 | tf_op jit(solution)/shard_map/ppermute | solution.py:351
  96.7 5.2 %collective-permute-start.31 = (f32[192,128]{1,0:T(8,128)S(1)}, f32[192,128]{1,0:T(8,128)S(1)}, u32[]{:S(2)}, u32[]{:S(2)}) collective-permute-start(f32[192,128]{1,0:T(8,128)S(1)} %add.34.refs_4_), channel_id=1, source_target_pairs={{0,4},{4,0},{8,12},{12,8},{16,20},{20,16},{24,28},{28,24},{1,5},{5... | collective-permute-start | bytes 294920 | tf_op jit(solution)/shard_map/ppermute | solution.py:351
  98.4 9.0 %copy-start = (f32[208,128]{1,0:T(8,128)}, f32[208,128]{1,0:T(8,128)S(1)}, u32[]{:S(2)}) copy-start(f32[208,128]{1,0:T(8,128)S(1)} %add.31.refs_0_) | copy-start | bytes 319492
  98.4 5.9 %collective-permute-start.36 = (f32[208,128]{1,0:T(8,128)S(1)}, f32[208,128]{1,0:T(8,128)S(1)}, u32[]{:S(2)}, u32[]{:S(2)}) collective-permute-start(f32[208,128]{1,0:T(8,128)S(1)} %add.31.refs_0_), channel_id=1, source_target_pairs={{0,24},{4,28},{8,16},{12,20},{16,8},{20,12},{24,0},{28,4},{1,25},{... | collective-permute-start | bytes 319496 | tf_op jit(solution)/shard_map/ppermute | solution.py:351
  100.2 7.2 %copy-start.17 = (f32[192,128]{1,0:T(8,128)}, f32[192,128]{1,0:T(8,128)S(1)}, u32[]{:S(2)}) copy-start(f32[192,128]{1,0:T(8,128)S(1)} %collective-permute-done.40.refs_14_) | copy-start | bytes 294916
  100.2 4.7 %collective-permute-start.34 = (f32[208,128]{1,0:T(8,128)S(1)}, f32[208,128]{1,0:T(8,128)S(1)}, u32[]{:S(2)}, u32[]{:S(2)}) collective-permute-start(f32[208,128]{1,0:T(8,128)S(1)} %add.31.refs_0_), channel_id=1, source_target_pairs={{0,8},{4,12},{8,0},{12,4},{16,24},{20,28},{24,16},{28,20},{1,9},{5... | collective-permute-start | bytes 319496 | tf_op jit(solution)/shard_map/ppermute | solution.py:351
  100.8 6.6 %copy-start.18 = (f32[192,128]{1,0:T(8,128)}, f32[192,128]{1,0:T(8,128)S(1)}, u32[]{:S(2)}) copy-start(f32[192,128]{1,0:T(8,128)S(1)} %collective-permute-done.38.refs_12_) | copy-start | bytes 294916
  100.8 4.7 %collective-permute-start.26 = (f32[208,128]{1,0:T(8,128)S(1)}, f32[208,128]{1,0:T(8,128)S(1)}, u32[]{:S(2)}, u32[]{:S(2)}) collective-permute-start(f32[208,128]{1,0:T(8,128)S(1)} %add.31.refs_0_), channel_id=1, source_target_pairs={{0,16},{4,20},{8,24},{12,28},{16,0},{20,4},{24,8},{28,12},{1,17},{... | collective-permute-start | bytes 319496 | tf_op jit(solution)/shard_map/ppermute | solution.py:351
  102.0 5.5 %copy-start.19 = (f32[192,128]{1,0:T(8,128)}, f32[192,128]{1,0:T(8,128)S(1)}, u32[]{:S(2)}) copy-start(f32[192,128]{1,0:T(8,128)S(1)} %collective-permute-done.32.refs_6_) | copy-start | bytes 294916
  102.0 3.6 %collective-permute-start.25 = (f32[208,128]{1,0:T(8,128)S(1)}, f32[208,128]{1,0:T(8,128)S(1)}, u32[]{:S(2)}, u32[]{:S(2)}) collective-permute-start(f32[208,128]{1,0:T(8,128)S(1)} %add.31.refs_0_), channel_id=1, source_target_pairs={{0,4},{4,0},{8,12},{12,8},{16,20},{20,16},{24,28},{28,24},{1,5},{5... | collective-permute-start | bytes 319496 | tf_op jit(solution)/shard_map/ppermute | solution.py:351
  102.0 5.5 %copy-start.20 = (f32[192,128]{1,0:T(8,128)}, f32[192,128]{1,0:T(8,128)S(1)}, u32[]{:S(2)}) copy-start(f32[192,128]{1,0:T(8,128)S(1)} %collective-permute-done.31.refs_5_) | copy-start | bytes 294916
  102.0 4.1 %collective-permute-start.41 = (f32[192,128]{1,0:T(8,128)S(1)}, f32[192,128]{1,0:T(8,128)S(1)}, u32[]{:S(2)}, u32[]{:S(2)}) collective-permute-start(f32[192,128]{1,0:T(8,128)S(1)} %collective-permute-done.40.refs_14_), channel_id=1, source_target_pairs={{0,4},{4,0},{8,12},{12,8},{16,20},{20,16},{24,28},{28,24},{1,5},{5... | collective-permute-start | bytes 294920 | tf_op jit(solution)/shard_map/ppermute | solution.py:351
  104.3 3.1 %copy-start.10 = (f32[208,128]{1,0:T(8,128)}, f32[208,128]{1,0:T(8,128)S(1)}, u32[]{:S(2)}) copy-start(f32[208,128]{1,0:T(8,128)S(1)} %collective-permute-done.36.refs_10_) | copy-start | bytes 319492
  104.3 3.0 %collective-permute-start.37 = (f32[208,128]{1,0:T(8,128)S(1)}, f32[208,128]{1,0:T(8,128)S(1)}, u32[]{:S(2)}, u32[]{:S(2)}) collective-permute-start(f32[208,128]{1,0:T(8,128)S(1)} %collective-permute-done.36.refs_10_), channel_id=1, source_target_pairs={{0,4},{4,0},{8,12},{12,8},{16,20},{20,16},{24,28},{28,24},{1,5},{5... | collective-permute-start | bytes 319496 | tf_op jit(solution)/shard_map/ppermute | solution.py:351
  104.9 2.6 %copy-start.11 = (f32[208,128]{1,0:T(8,128)}, f32[208,128]{1,0:T(8,128)S(1)}, u32[]{:S(2)}) copy-start(f32[208,128]{1,0:T(8,128)S(1)} %collective-permute-done.34.refs_8_) | copy-start | bytes 319492
  104.9 2.5 %collective-permute-start.35 = (f32[208,128]{1,0:T(8,128)S(1)}, f32[208,128]{1,0:T(8,128)S(1)}, u32[]{:S(2)}, u32[]{:S(2)}) collective-permute-start(f32[208,128]{1,0:T(8,128)S(1)} %collective-permute-done.34.refs_8_), channel_id=1, source_target_pairs={{0,4},{4,0},{8,12},{12,8},{16,20},{20,16},{24,28},{28,24},{1,5},{5... | collective-permute-start | bytes 319496 | tf_op jit(solution)/shard_map/ppermute | solution.py:351
  105.5 1.9 %copy-start.12 = (f32[208,128]{1,0:T(8,128)}, f32[208,128]{1,0:T(8,128)S(1)}, u32[]{:S(2)}) copy-start(f32[208,128]{1,0:T(8,128)S(1)} %collective-permute-done.26.refs_2_) | copy-start | bytes 319492
  105.5 1.9 %collective-permute-start.27 = (f32[208,128]{1,0:T(8,128)S(1)}, f32[208,128]{1,0:T(8,128)S(1)}, u32[]{:S(2)}, u32[]{:S(2)}) collective-permute-start(f32[208,128]{1,0:T(8,128)S(1)} %collective-permute-done.26.refs_2_), channel_id=1, source_target_pairs={{0,4},{4,0},{8,12},{12,8},{16,20},{20,16},{24,28},{28,24},{1,5},{5... | collective-permute-start | bytes 319496 | tf_op jit(solution)/shard_map/ppermute | solution.py:351
  105.5 1.4 %collective-permute-start.39 = (f32[192,128]{1,0:T(8,128)S(1)}, f32[192,128]{1,0:T(8,128)S(1)}, u32[]{:S(2)}, u32[]{:S(2)}) collective-permute-start(f32[192,128]{1,0:T(8,128)S(1)} %collective-permute-done.38.refs_12_), channel_id=1, source_target_pairs={{0,4},{4,0},{8,12},{12,8},{16,20},{20,16},{24,28},{28,24},{1,5},{5... | collective-permute-start | bytes 294920 | tf_op jit(solution)/shard_map/ppermute | solution.py:351
  106.0 1.3 %collective-permute-start.33 = (f32[192,128]{1,0:T(8,128)S(1)}, f32[192,128]{1,0:T(8,128)S(1)}, u32[]{:S(2)}, u32[]{:S(2)}) collective-permute-start(f32[192,128]{1,0:T(8,128)S(1)} %collective-permute-done.32.refs_6_), channel_id=1, source_target_pairs={{0,4},{4,0},{8,12},{12,8},{16,20},{20,16},{24,28},{28,24},{1,5},{5... | collective-permute-start | bytes 294920 | tf_op jit(solution)/shard_map/ppermute | solution.py:351
  (15 other events, 13.0 us)
